TPU v7x, 768 devices: a whole 4x8x12 slice. The times are simulated.
768 devices in a mesh: row: 64 (over x, y, core), col: 12 (over z).
Axes of the slice: x: 4, y: 8, z: 12, core: 2. Of those that a mesh axis runs over, the one named last changes fastest.
Arguments:
- matrix: float32 [12, 64, 16, 12288], P(None, 'row', None, 'col'), may hold values from -6 to 6
- panel: float32 [12, 64, 16, 384], P(None, 'row'), may hold values from -500 to 500
Outputs:
- updated: float32 [12, 64, 16, 12288], P(None, 'row', None, 'col')
All inputs are finite; a program needn't handle non-finite values.
Results may differ from a plain program's by a relative error of at most 0.00005.
Values sent between devices are 32-bit elements; how exact they have to be, the bound alone decides.
A program may use at most 64 MiB of HBM per device.

v0:
```python
import jax
import jax.numpy as jnp
from jax import lax
from jax.sharding import PartitionSpec as P

exact_mode = lax.Precision.HIGHEST


def over_pieces(shard, axis):
    return lax.all_gather(shard, axis).sum(0)


def plain_product(left, right):
    return jnp.dot(left, right, precision=exact_mode, preferred_element_type=jnp.float32)


def transposed_product(left, right):
    return lax.dot_general(
        left,
        right,
        (((0,), (0,)), ((), ())),
        precision=exact_mode,
        preferred_element_type=jnp.float32,
    )


def product_with_transpose(left, right):
    return lax.dot_general(
        left,
        right,
        (((1,), (1,)), ((), ())),
        precision=exact_mode,
        preferred_element_type=jnp.float32,
    )


def factor_inverse(gram):
    lower_factor = jnp.linalg.cholesky(gram)
    identity_matrix = jnp.eye(gram.shape[0], dtype=gram.dtype)
    return lax.linalg.triangular_solve(lower_factor, identity_matrix, left_side=True, lower=True)


def per_device(matrix, panel):
    rounds = matrix.shape[0]
    tile_rows = matrix.shape[2]
    width = matrix.shape[3]
    panel_width = panel.shape[3]
    row_count = lax.axis_size("row")
    col_count = lax.axis_size("col")
    row_index = lax.axis_index("row")
    col_index = lax.axis_index("col")
    per_block = rounds // col_count
    local_rows = rounds * tile_rows
    round_ids = lax.broadcasted_iota(jnp.int32, (rounds, tile_rows, width), 0)
    within_ids = lax.broadcasted_iota(jnp.int32, (rounds, tile_rows, width), 1)
    column_ids = lax.broadcasted_iota(jnp.int32, (rounds, tile_rows, width), 2) + col_index * width
    global_rows = (round_ids * row_count + row_index) * tile_rows + within_ids
    local_tile = matrix.reshape(rounds, tile_rows, width)
    half_tile = jnp.where(
        global_rows > column_ids,
        local_tile,
        jnp.where(global_rows == column_ids, 0.5 * local_tile, 0.0),
    )
    half_lower = half_tile.reshape(local_rows, width)
    panel_rows = panel.reshape(local_rows, panel_width)
    slot_start = col_index * per_block
    by_block = half_tile.reshape(col_count, per_block, tile_rows, per_block, row_count, tile_rows)
    strips = lax.all_to_all(by_block, "col", split_axis=0, concat_axis=0, tiled=True)
    received = lax.all_to_all(strips, "row", split_axis=4, concat_axis=4, tiled=True)

    def across_rows(values):
        own_part = lax.dynamic_slice_in_dim(values, slot_start, per_block, 0)
        gathered = lax.all_gather(own_part[:, None], "row", axis=1, tiled=True)
        return gathered.reshape(width, panel_width)

    gram = lax.psum(transposed_product(panel_rows, panel_rows), "row")
    inverse_factor = factor_inverse(gram)
    basis_rows = product_with_transpose(panel_rows, inverse_factor)
    basis_cols = across_rows(basis_rows.reshape(rounds, tile_rows, panel_width))
    direct_terms = plain_product(half_lower, basis_cols)
    partial_image = direct_terms.reshape(rounds, tile_rows, panel_width)
    basis_view = basis_cols.reshape(per_block, row_count, tile_rows, panel_width)
    mirror_terms = jnp.einsum(
        "xuwqvs,uvwb->xqsb",
        received,
        basis_view,
        precision=exact_mode,
        preferred_element_type=jnp.float32,
    )
    partial_image = partial_image + mirror_terms.reshape(rounds, tile_rows, panel_width)
    image_blocks = over_pieces(partial_image, "col")
    image_cols = across_rows(image_blocks)
    image_rows = image_blocks.reshape(local_rows, panel_width)
    curvature = lax.psum(transposed_product(basis_cols, image_cols), "col")
    residual_rows = image_rows - plain_product(basis_rows, curvature)
    residual_cols = image_cols - plain_product(basis_cols, curvature)
    change = product_with_transpose(basis_rows, residual_cols) + product_with_transpose(
        residual_rows, basis_cols
    )
    changed = local_tile - 2.0 * change.reshape(rounds, tile_rows, width)
    result = jnp.where(global_rows >= column_ids, changed, 0.0)
    return result.reshape(rounds, 1, tile_rows, width)


def solution(mesh):
    in_specs = (P(None, "row", None, "col"), P(None, "row", None, None))
    out_specs = P(None, "row", None, "col")
    return jax.shard_map(
        per_device, mesh=mesh, in_specs=in_specs, out_specs=out_specs, check_vma=False
    )
```

profile of v0, /device:TPU:1, one launch (start us, length us, event | category | flops | bytes accessed | tf_op | source)
XLA Modules:
  0.0 705.6 jit_solution(15671820594441943665)
XLA Ops:
  6.5 1.0 copy-done
  7.5 1.7 convolution_bitcast_fusion.1
  9.3 4.1 reshape.164
  13.4 7.1 %select_select_fusion = f32[12,1,16,1,64,16]{5,4,2,0,3,1:T(8,128)} fusion(f32[12,1,16,1,64,16]{5,4,2,0,3,1:T(8,128)} %reshape.164, s32[64,16]{1,0:T(8,128)S(1)} %add_add_fusion, s32[12]{0:T(128)S(1)} %add_multiply_fusion), kind=kLoop, calls=%fused_computation.2 | loop fusion | flops 1179648 | bytes 1577008 | tf_op jit(solution)/shard_map/jit(_where)/select_n | solution.py:59
  20.5 4.4 copy.19
  24.9 1.9 reshape.201
  26.8 15.7 %all-to-all-start = ((f32[12,1,16384]{2,1,0:T(1,128)}), f32[12,1,16384]{2,1,0:T(1,128)S(1)}, u32[]{:S(2)}, u32[]{:S(2)}) async-start(f32[12,1,16384]{2,1,0:T(1,128)} %reshape.201), calls=%async_computation | async-start | bytes 1572864 | tf_op jit(solution)/shard_map/all_to_all | solution.py:68
  42.5 0.3 all-gather.7.cloned.1.call-start
  42.8 0.9 fusion.38
  43.7 178.0 %all-reduce.4.cloned.1.call-done = f32[384,384]{0,1:T(8,128)} async-done(((f32[384,384]{0,1:T(8,128)}), f32[384,384]{0,1:T(8,128)}) %all-reduce.4.cloned.1.call-update) | async-done | bytes 589840 | tf_op jit(solution)/shard_map/psum | solution.py:76
  221.7 1.4 copy.18
  223.1 0.8 copy-done.5
  223.9 11.7 %cholesky.77 = f32[128,128]{1,0:T(8,128)S(1)} custom-call(f32[128,128]{1,0:T(8,128)S(1)} %cholesky.192), custom_call_target="Cholesky" | custom-call | tf_op jit(solution)/shard_map/jit(cholesky)/cholesky | solution.py:38
  235.7 9.8 %custom-call.22 = f32[1,128,128]{1,2,0:T(8,128)S(1)} custom-call(f32[1,128,128]{2,1,0:T(8,128)S(1)} %get-tuple-element.29), custom_call_target="InvertDiagBlocksLowerTriangular" | custom-call | tf_op jit(solution)/shard_map/jit(cholesky)/cholesky | solution.py:38
  245.5 1.2 constant_dynamic-update-slice_fusion.1
  246.7 1.2 convolution_subtract_fusion.3
  247.9 11.7 %cholesky.162 = f32[128,128]{1,0:T(8,128)S(1)} custom-call(f32[128,128]{1,0:T(8,128)S(1)} %cholesky.196), custom_call_target="Cholesky" | custom-call | tf_op jit(solution)/shard_map/jit(cholesky)/cholesky | solution.py:38
  259.7 10.2 %custom-call.23 = f32[1,128,128]{1,2,0:T(8,128)S(1)} custom-call(f32[1,128,128]{2,1,0:T(8,128)S(1)} %get-tuple-element.26), custom_call_target="InvertDiagBlocksLowerTriangular" | custom-call | tf_op jit(solution)/shard_map/jit(cholesky)/cholesky | solution.py:38
  269.8 0.2 convolution_dynamic-update-slice_fusion
  270.1 1.1 convolution_subtract_fusion.4
  271.2 11.7 %cholesky.181 = f32[128,128]{1,0:T(8,128)S(1)} custom-call(f32[128,128]{1,0:T(8,128)S(1)} %convolution_subtract_fusion.4), custom_call_target="Cholesky" | custom-call | tf_op jit(solution)/shard_map/jit(cholesky)/cholesky | solution.py:38
  282.9 0.7 compare_reduce_fusion
  283.6 0.7 compare_reduce_fusion.1
  286.3 8.2 %while.1 = (s32[]{:T(128)}, f32[384,384]{1,0:T(8,128)S(1)}, s32[3,2]{0,1:T(2,128)S(1)}, f32[3,128,128]{2,1,0:T(8,128)}, s32[]{:T(128)}) while((s32[]{:T(128)}, f32[384,384]{1,0:T(8,128)S(1)}, s32[3,2]{0,1:T(2,128)S(1)}, f32[3,128,128]{2,1,0:T(8,128)}, s32[]{:T(128)}) %tuple.25), condition=%wide.while_cond, body=%wide.while_body.sunk | while | flops 2 | bytes 132705 | solution.py:40
  286.4 0.6 fusion.73
  287.0 2.1 bitcast_dynamic-update-slice_fusion.2
  289.1 0.6 fusion.73
  289.7 2.1 bitcast_dynamic-update-slice_fusion.2
  291.9 0.6 fusion.73
  292.5 2.1 bitcast_dynamic-update-slice_fusion.2
  294.5 30.3 %custom-call.24 = f32[3,128,128]{1,2,0:T(8,128)S(1)} custom-call(f32[3,128,128]{2,1,0:T(8,128)} %get-tuple-element.12), custom_call_target="InvertDiagBlocksLowerTriangular" | custom-call | tf_op jit(solution)/shard_map/triangular_solve | solution.py:40
  324.8 0.3 fusion.36
  325.1 1.2 convolution_subtract_fusion.2
  326.4 0.4 fusion.45
  326.8 1.3 convolution_subtract_fusion.1
  328.1 1.2 fusion.43
  329.3 0.8 fusion.21
  330.1 0.6 constant_dynamic-slice_fusion.2
  330.8 0.5 broadcast.295
  331.3 3.7 reduce.18
  335.0 1.8 reshape.202
  336.9 6.1 copy.20
  343.0 5.5 reshape.203
  348.5 9.8 %all-to-all-start.1 = ((f32[64,1,3072]{2,1,0:T(1,128)}), f32[64,1,3072]{2,1,0:T(1,128)S(1)}, u32[]{:S(2)}, u32[]{:S(2)}) async-start(f32[64,1,3072]{2,1,0:T(1,128)} %reshape.203), calls=%async_computation.1 | async-start | bytes 1572864 | tf_op jit(solution)/shard_map/all_to_all | solution.py:69
  358.3 0.2 all-gather.9.cloned.1.call-start
  358.5 23.2 %all-to-all-done.1 = f32[64,1,3072]{2,1,0:T(1,128)S(1)} async-done(((f32[64,1,3072]{2,1,0:T(1,128)}), f32[64,1,3072]{2,1,0:T(1,128)S(1)}, u32[]{:S(2)}, u32[]{:S(2)}) %all-to-all-start.1) | async-done | bytes 786464 | tf_op jit(solution)/shard_map/all_to_all | solution.py:69
  381.8 2.5 reduce.19
  384.3 3.8 reshape.204
  388.1 6.3 copy.21
  394.4 27.4 %all-gather.7.cloned.1.call-done = f32[64,16,384]{2,1,0:T(8,128)} async-done(((f32[1,16,384]{2,1,0:T(8,128)}), f32[64,16,384]{2,1,0:T(8,128)}) %all-gather.7.cloned.1.call-update) | async-done | bytes 1572880 | tf_op jit(solution)/shard_map/all_gather | solution.py:73
  421.8 4.0 fusion.7
  425.9 2.3 convolution_add_fusion.1
  428.3 57.5 %all-gather.9.cloned.1.call-done = f32[144,16,384]{2,1,0:T(8,128)} async-done(((f32[12,16,384]{2,1,0:T(8,128)}), f32[144,16,384]{2,1,0:T(8,128)}) %all-gather.9.cloned.1.call-update) | async-done | bytes 3538960 | tf_op jit(solution)/shard_map/all_gather | solution.py:10
  485.8 2.2 reduce_sum.9
  488.0 0.6 constant_dynamic-slice_fusion.1
  488.6 0.3 all-reduce.6.cloned.1.call-start
  488.9 90.9 %all-gather.11.cloned.1.call-done = f32[64,16,384]{2,1,0:T(8,128)} async-done(((f32[1,16,384]{2,1,0:T(8,128)}), f32[64,16,384]{2,1,0:T(8,128)}) %all-gather.11.cloned.1.call-update) | async-done | bytes 1572880 | tf_op jit(solution)/shard_map/all_gather | solution.py:73
  579.8 4.9 convolution_bitcast_fusion
  584.7 103.7 %all-reduce.6.cloned.1.call-done = f32[384,384]{1,0:T(8,128)} async-done(((f32[384,384]{1,0:T(8,128)}), f32[384,384]{1,0:T(8,128)}) %all-reduce.6.cloned.1.call-update) | async-done | bytes 589840 | tf_op jit(solution)/shard_map/psum | solution.py:94
  688.4 4.8 bitcast_subtract_fusion
  693.2 2.0 fusion.55
  695.2 0.8 convolution_subtract_fusion
  695.9 1.9 fusion.6
  697.8 1.1 subtract_select_fusion
  (38 shorter events, 0.7 us)
Async XLA Ops:
  6.5 1.0 copy-start
  6.5 2.8 copy-start.2
  6.5 215.1 %all-reduce.4.cloned.1.call-start = ((), (), s32[]{:S(2)}) async-start(), calls=%async_computation.2 | async-start | bytes 1179648 | tf_op jit(solution)/shard_map/psum | solution.py:76
  26.8 304.0 %all-to-all-start = ((f32[12,1,16384]{2,1,0:T(1,128)}), f32[12,1,16384]{2,1,0:T(1,128)S(1)}, u32[]{:S(2)}, u32[]{:S(2)}) async-start(f32[12,1,16384]{2,1,0:T(1,128)} %reshape.201), calls=%async_computation | async-start | bytes 1572864 | tf_op jit(solution)/shard_map/all_to_all | solution.py:68
  42.5 379.3 %all-gather.7.cloned.1.call-start = ((), (), s32[]{:S(2)}) async-start(), calls=%async_computation.4 | async-start | bytes 1597440 | tf_op jit(solution)/shard_map/all_gather | solution.py:73
  221.7 1.4 copy-start.3
  223.1 0.8 copy-start.5
  324.8 1.6 copy-start.6
  348.5 33.3 %all-to-all-start.1 = ((f32[64,1,3072]{2,1,0:T(1,128)}), f32[64,1,3072]{2,1,0:T(1,128)S(1)}, u32[]{:S(2)}, u32[]{:S(2)}) async-start(f32[64,1,3072]{2,1,0:T(1,128)} %reshape.203), calls=%async_computation.1 | async-start | bytes 1572864 | tf_op jit(solution)/shard_map/all_to_all | solution.py:69
  358.3 127.5 %all-gather.9.cloned.1.call-start = ((), (), s32[]{:S(2)}) async-start(), calls=%async_computation.5 | async-start | bytes 3833856 | tf_op jit(solution)/shard_map/all_gather | solution.py:10
  421.8 4.0 copy-start.1
  428.2 151.6 %all-gather.11.cloned.1.call-start = ((), (), s32[]{:S(2)}) async-start(), calls=%async_computation.6 | async-start | bytes 1597440 | tf_op jit(solution)/shard_map/all_gather | solution.py:73
  488.6 199.7 %all-reduce.6.cloned.1.call-start = ((), (), s32[]{:S(2)}) async-start(), calls=%async_computation.3 | async-start | bytes 1179648 | tf_op jit(solution)/shard_map/psum | solution.py:94
  693.2 2.0 copy-start.4
Sparse Core Ops, SparseCore 0:
  10.8 210.8 all-reduce.3
  330.9 90.8 all-gather.6
  428.3 57.3 all-gather.8
  489.5 90.1 all-gather.10
  584.8 103.5 all-reduce.5
where the time goes:
time: 717 us; the launch traced here: 706 us
  waiting for transfers between devices  481 us (67%)
  other arithmetic  105 us (15%)
  local copies, waits for them, and re-layouts  47.1 us (7%)
  matrix products  31.2 us (4%)
  starting transfers between devices  26.3 us (4%)
  between operations  15.7 us (2%)
    psum x1, waiting for transfers between devices, per_device(): gram = lax.psum(transposed_product(panel_rows, panel_rows), 'row')  178 us
    all_gather x2, waiting for transfers between devices, across_rows(): gathered = lax.all_gather(own_part[:, None], 'row', axis=1, tiled=True)  118 us
    psum x1, waiting for transfers between devices, per_device(): curvature = lax.psum(transposed_product(basis_cols, image_cols), 'col')  104 us
    all_gather x1, waiting for transfers between devices, over_pieces(): return lax.all_gather(shard, axis).sum(0)  57.5 us
    another operation x10, other arithmetic, factor_inverse(): lower_factor = jnp.linalg.cholesky(gram)  56.6 us
    another operation x3, other arithmetic, factor_inverse(): lax.linalg.triangular_solve(lower_factor, identity_matrix, left_side=True...  30.4 us
    all_to_all x1, waiting for transfers between devices, per_device(): lax.all_to_all(strips, 'row', split_axis=4, concat_axis=4, tiled=True)  23.2 us
    all_to_all x1, starting transfers between devices, per_device(): lax.all_to_all(by_block, 'col', split_axis=0, concat_axis=0, tiled=True)  15.7 us
  transfers between devices with their start and end apart: 7, of which 6 were waited for; matrix products, arithmetic and copies ran while one was open for 22% of the time, Pallas kernels for 0%

commit v1 on v0

v1 whole, which is shorter than its diff:
```python
import functools

import jax
import jax.numpy as jnp
from jax import lax
from jax.experimental import pallas as pl
from jax.experimental.pallas import tpu as pltpu
from jax.sharding import PartitionSpec as P

EXACT = lax.Precision.HIGHEST
PLANES = {64: (4, 8), 8: (2, 2)}


def dot_nn(a, b):
    return lax.dot_general(a, b, (((1,), (0,)), ((), ())), precision=EXACT,
                           preferred_element_type=jnp.float32)


def dot_tn(a, b):
    return lax.dot_general(a, b, (((0,), (0,)), ((), ())), precision=EXACT,
                           preferred_element_type=jnp.float32)


def dot_nt(a, b):
    return lax.dot_general(a, b, (((1,), (1,)), ((), ())), precision=EXACT,
                           preferred_element_type=jnp.float32)


def by_distance(n):
    return sorted(range(1, n), key=lambda d: (min(d, n - d), d))


def comm_kernel(sizes, mat_ref, pan_ref, g_ref, k_ref, tc_ref, wc_ref, wr_ref,
                h_ref, gl_ref, gc_ref, gsum_ref, gx_ref, gsx_ref, gy_ref, gf_ref,
                mp_ref, cx_ref, mx_ref, ms_ref, my_ref,
                dp_ref, rz_ref, kp_ref, kc_ref, kx_ref, ks_ref, ky_ref, kz_ref, kf_ref,
                send_sems, t_sems, w_sems, wz_sems, mc_sems, mx_sems, my_sems, dz_sems,
                g_sems, gz_sems, k_sems, kz_sems, ka_sems):
    NX, NY, NZ, TR, WIDTH, PW = sizes
    row = lax.axis_index("row")
    z = lax.axis_index("col")
    core = lax.rem(row, 2)
    chip = lax.div(row, 2)
    y = lax.rem(chip, NY)
    x = lax.div(chip, NY)
    other = 1 - core

    def at(x_, y_, c_):
        return (x_ * NY + y_) * 2 + c_

    def xp(d):
        return lax.rem(x + d, NX)

    def yp(d):
        return lax.rem(y + d, NY)

    def zp(d):
        return lax.rem(z + d, NZ)

    to_x = lambda d: (at(xp(d), y, core), z)
    to_y = lambda d: (at(x, yp(d), core), z)
    to_z = lambda d: (row, zp(d))
    to_core = (at(x, y, other), z)

    barrier = pltpu.get_barrier_semaphore()
    peers = ([to_x(d) for d in range(1, NX)] + [to_y(d) for d in range(1, NY)]
             + [to_z(d) for d in range(1, NZ)] + [to_core])
    for peer in peers:
        pl.semaphore_signal(barrier, inc=1, device_id=peer, device_id_type=pl.DeviceIdType.MESH)
    pl.semaphore_wait(barrier, len(peers))

    sent = []

    def send(src, dst, sem, peer, when=None):
        slot = len(sent)
        sent.append((src, when))
        pltpu.make_async_remote_copy(
            src_ref=src, dst_ref=dst, send_sem=send_sems.at[slot], recv_sem=sem,
            device_id=peer, device_id_type=pl.DeviceIdType.MESH).start()

    def left(slot, src):
        pltpu.make_async_remote_copy(
            src_ref=src, dst_ref=src, send_sem=send_sems.at[slot], recv_sem=t_sems.at[0],
            device_id=to_core, device_id_type=pl.DeviceIdType.MESH).wait_send()

    def arrive(dst, sem):
        pltpu.make_async_remote_copy(
            src_ref=dst, dst_ref=dst, send_sem=send_sems.at[0], recv_sem=sem,
            device_id=to_core, device_id_type=pl.DeviceIdType.MESH).wait_recv()

    YD, XD, ZD = by_distance(NY), by_distance(NX), by_distance(NZ)

    own_t = pan_ref.at[z]
    for d in YD:
        send(own_t, tc_ref.at[x, y, core], t_sems.at[row], to_y(d))
    for d in XD:
        send(own_t, tc_ref.at[x, y, core], t_sems.at[row], to_x(d))
    tc_ref[x, y, core] = pan_ref[z]

    t_rows = pan_ref[...].reshape(NZ * TR, PW)
    gl_ref[...] = dot_tn(t_rows, t_rows).reshape(NZ, 2, PW // NZ // 2, PW)
    send(gl_ref.at[z, other], gc_ref, g_sems.at[0], to_core)

    sub = lax.broadcasted_iota(jnp.int32, (TR, WIDTH), 0) + row * TR
    lane = lax.broadcasted_iota(jnp.int32, (TR, WIDTH), 1)
    weight_diag = jnp.where(sub > lane, 1.0, jnp.where(sub == lane, 0.5, 0.0))
    for a in range(NZ):
        tile = mat_ref[a]
        diag_part = jnp.where(weight_diag > 0.0, tile * weight_diag, 0.0)
        h_ref[a] = jnp.where(z < a, tile, jnp.where(z == a, diag_part, 0.0))

    XW = WIDTH // NX
    for d in list(XD) + [0]:
        xb = xp(d)
        cols = pl.ds(pl.multiple_of(xb * XW, XW), XW)
        h = h_ref[:, :, cols].reshape(NZ * TR, XW)
        mp_ref[xb] = dot_tn(h, t_rows).reshape(NY, 2, TR, PW)
        send(mp_ref.at[xb, :, other], cx_ref.at[xb], mc_sems.at[xb], to_core)

    arrive(gc_ref, g_sems.at[0])
    gsum_ref[...] = gl_ref[z, core] + gc_ref[...]
    for d in XD:
        send(gsum_ref, gx_ref.at[d - 1], g_sems.at[d], to_x(d))

    for d in list(XD) + [0]:
        xb = xp(d)
        arrive(cx_ref.at[xb], mc_sems.at[xb])
        ms_ref[xb] = mp_ref[xb, :, core] + cx_ref[xb]
        if d:
            send(ms_ref.at[xb], mx_ref.at[d - 1], mx_sems.at[d - 1], to_x(d))

    for d in YD:
        tile = tc_ref.at[x, yp(NY - d), core]
        sem = t_sems.at[at(x, yp(NY - d), core)]
        arrive(tile, sem)
        for dx in XD:
            send(tile, tile, sem, to_x(dx))

    TS = NX * NY * 2

    send(tc_ref.at[x, :, core], tc_ref.at[x, :, core], t_sems.at[TS + x], to_core)

    gs = gsum_ref[...]
    for d in XD:
        arrive(gx_ref.at[d - 1], g_sems.at[d])
        gs = gs + gx_ref[d - 1]
    gsx_ref[...] = gs
    for d in YD:
        send(gsx_ref, gy_ref.at[d - 1], g_sems.at[NX + d], to_y(d))

    for dx in XD:
        xb = xp(NX - dx)
        for dy in [0] + YD:
            arrive(tc_ref.at[xb, yp(NY - dy), core], t_sems.at[at(xb, yp(NY - dy), core)])
        send(tc_ref.at[xb, :, core], tc_ref.at[xb, :, core], t_sems.at[TS + xb], to_core)

    for d in XD:
        arrive(mx_ref.at[d - 1], mx_sems.at[d - 1])
    msum = ms_ref[x]
    for d in XD:
        msum = msum + mx_ref[d - 1]
    mp_ref[x, :, core] = msum
    for d in YD:
        send(mp_ref.at[x, yp(d), core], my_ref.at[d - 1], my_sems.at[d - 1], to_y(d))

    for dx in [0] + XD:
        xb = xp(NX - dx)
        arrive(tc_ref.at[xb, :, other], t_sems.at[TS + xb])

    direct = dot_nn(h_ref[...].reshape(NZ * TR, WIDTH), tc_ref[...].reshape(WIDTH, PW))
    dp_ref[...] = direct.reshape(NZ, TR, PW)
    for d in ZD:
        send(dp_ref.at[zp(d)], rz_ref.at[d - 1], dz_sems.at[d - 1], to_z(d))
    NP = PW // 2 // NX // 8
    kp_ref[...] = dot_tn(t_rows, direct).reshape(2, NX, NP, 8, PW)
    send(kp_ref.at[other], kc_ref, k_sems.at[0], to_core)

    gs = gsx_ref[...]
    for d in YD:
        arrive(gy_ref.at[d - 1], g_sems.at[NX + d])
        gs = gs + gy_ref[d - 1]
    gf_ref[...] = gs
    g_ref[z, core] = gs
    for d in ZD:
        send(gf_ref, g_ref.at[z, core], gz_sems.at[d - 1], to_z(d))

    msum = mp_ref[x, y, core]
    for d in YD:
        arrive(my_ref.at[d - 1], my_sems.at[d - 1])
        msum = msum + my_ref[d - 1]

    arrive(kc_ref, k_sems.at[0])
    ks_ref[...] = kp_ref[core] + kc_ref[...]
    for d in XD:
        send(ks_ref.at[xp(d)], kx_ref.at[d - 1], k_sems.at[d], to_x(d))

    wsum = msum + dp_ref[z]
    for d in ZD:
        arrive(rz_ref.at[d - 1], dz_sems.at[d - 1])
        wsum = wsum + rz_ref[d - 1]
    wc_ref[x, y, core] = wsum
    wr_ref[z] = wsum
    for d in YD:
        send(wc_ref.at[x, y, core], wc_ref.at[x, y, core], w_sems.at[row], to_y(d))
    for d in XD:
        send(wc_ref.at[x, y, core], wc_ref.at[x, y, core], w_sems.at[row], to_x(d))
    for d in ZD:
        send(wr_ref.at[z], wr_ref.at[z], wz_sems.at[d - 1], to_z(d))

    for d in XD:
        arrive(kx_ref.at[d - 1], k_sems.at[d])
    ksum = ks_ref[x]
    for d in XD:
        ksum = ksum + kx_ref[d - 1]
    ks_ref[x] = ksum
    for d in YD:
        piece = ks_ref.at[x, lax.min(yp(d), NP - 1)]
        goes = yp(d) < NP

        @pl.when(goes)
        def _():
            send(piece, ky_ref.at[d - 1], k_sems.at[NX + d], to_y(d), goes)

    for d in YD:
        tile = wc_ref.at[x, yp(NY - d), core]
        sem = w_sems.at[at(x, yp(NY - d), core)]
        arrive(tile, sem)
        for dx in XD:
            send(tile, tile, sem, to_x(dx))
    send(wc_ref.at[x, :, core], wc_ref.at[x, :, core], w_sems.at[TS + x], to_core)

    held = y < NP
    yy = lax.min(y, NP - 1)

    @pl.when(held)
    def _():
        ksum = ks_ref[x, yy]
        for d in YD:
            arrive(ky_ref.at[d - 1], k_sems.at[NX + d])
            ksum = ksum + ky_ref[d - 1]
        kf_ref[...] = ksum
        for d in ZD:
            send(kf_ref, kz_ref.at[d - 1], kz_sems.at[d - 1], to_z(d), held)

    for d in ZD:
        src_z = zp(NZ - d)
        arrive(g_ref.at[src_z, core], gz_sems.at[d - 1])
    send(g_ref.at[:, core], g_ref.at[:, core], g_sems.at[NX + NY], to_core)

    for dx in XD:
        xb = xp(NX - dx)
        for dy in [0] + YD:
            arrive(wc_ref.at[xb, yp(NY - dy), core], w_sems.at[at(xb, yp(NY - dy), core)])
        send(wc_ref.at[xb, :, core], wc_ref.at[xb, :, core], w_sems.at[TS + xb], to_core)

    own_k = k_ref.at[core, x, yy]
    @pl.when(held)
    def _():
        ksum = kf_ref[...]
        for d in ZD:
            arrive(kz_ref.at[d - 1], kz_sems.at[d - 1])
            ksum = ksum + kz_ref[d - 1]
        k_ref[core, x, yy] = ksum
        for d in YD:
            send(own_k, own_k, ka_sems.at[d], to_y(d), held)

    for d in YD:
        src_y = yp(NY - d)

        @pl.when(src_y < NP)
        def _():
            piece = k_ref.at[core, x, lax.min(src_y, NP - 1)]
            arrive(piece, ka_sems.at[d])
    for d in XD:
        send(k_ref.at[core, x], k_ref.at[core, x], ka_sems.at[NY + d], to_x(d))
    for d in XD:
        arrive(k_ref.at[core, xp(NX - d)], ka_sems.at[NY + d])
    send(k_ref.at[core], k_ref.at[core], ka_sems.at[0], to_core)

    for d in ZD:
        arrive(wr_ref.at[zp(NZ - d)], wz_sems.at[d - 1])
    arrive(g_ref.at[:, other], g_sems.at[NX + NY])
    for dx in [0] + XD:
        xb = xp(NX - dx)
        arrive(wc_ref.at[xb, :, other], w_sems.at[TS + xb])
    arrive(k_ref.at[other], ka_sems.at[0])
    for slot, (src, when) in enumerate(sent):
        if when is None:
            left(slot, src)
        else:
            pl.when(when)(functools.partial(left, slot, src))


def exchange(matrix, panel, sizes):
    NX, NY, NZ, TR, WIDTH, PW = sizes
    f32 = jnp.float32
    TS = NX * NY * 2
    NP = PW // 2 // NX // 8
    GR = PW // NZ // 2
    vmem = pl.BlockSpec(memory_space=pltpu.VMEM)
    shape = lambda *s: jax.ShapeDtypeStruct(s, f32)
    V = lambda *s: pltpu.VMEM(s, f32)
    D = lambda n: pltpu.SemaphoreType.DMA((n,))
    return pl.pallas_call(
        functools.partial(comm_kernel, sizes),
        out_shape=[shape(NZ, 2, GR, PW), shape(2, NX, NP, 8, PW), shape(NX, NY, 2, TR, PW),
                   shape(NX, NY, 2, TR, PW), shape(NZ, TR, PW)],
        in_specs=[vmem, vmem],
        out_specs=[vmem] * 5,
        scratch_shapes=[
            V(NZ, TR, WIDTH), V(NZ, 2, GR, PW), V(GR, PW), V(GR, PW), V(NX - 1, GR, PW), V(GR, PW),
            V(NY - 1, GR, PW), V(GR, PW),
            V(NX, NY, 2, TR, PW), V(NX, NY, TR, PW), V(NX - 1, NY, TR, PW), V(NX, NY, TR, PW),
            V(NY - 1, TR, PW),
            V(NZ, TR, PW), V(NZ - 1, TR, PW), V(2, NX, NP, 8, PW), V(NX, NP, 8, PW),
            V(NX - 1, NP, 8, PW), V(NX, NP, 8, PW), V(NY - 1, 8, PW), V(NZ - 1, 8, PW), V(8, PW),
            D(200), D(TS + NX), D(TS + NX), D(NZ - 1), D(NX), D(NX - 1), D(NY - 1), D(NZ - 1),
            D(NX + NY + 1), D(NZ - 1), D(NX + NY), D(NZ - 1), D(NX + NY),
        ],
        compiler_params=pltpu.CompilerParams(
            collective_id=0, has_side_effects=True, vmem_limit_bytes=32 * 2**20),
        name="exchange",
    )(matrix, panel)


def inverse(gram):
    n = gram.shape[0]
    ids_r = lax.broadcasted_iota(jnp.int32, (n, n), 0)
    ids_c = lax.broadcasted_iota(jnp.int32, (n, n), 1)
    eye = jnp.where(ids_r == ids_c, 1.0, 0.0)
    diag = gram * eye
    s_row = lax.rsqrt(jnp.sum(diag, axis=0, keepdims=True))
    s_col = lax.rsqrt(jnp.sum(diag, axis=1, keepdims=True))
    scaled = gram * s_row * s_col
    bound = jnp.max(jnp.sum(jnp.abs(scaled), axis=0, keepdims=True))
    start = eye * (2.0 / (1.0 + bound))

    def step(state):
        count, _, guess = state
        residual = eye - dot_nn(scaled, guess)
        error = jnp.sum(residual * residual)
        return count + 1, error, guess + dot_nn(guess, residual)

    def again(state):
        return jnp.logical_and(state[1] > 1e-8, state[0] < 80)

    _, _, found = lax.while_loop(again, step, (0, jnp.float32(1.0), start))
    return found * s_row * s_col


def finish_kernel(mat_ref, pan_ref, g_ref, k_ref, tc_ref, wc_ref, wr_ref, out_ref):
    NZ, TR, WIDTH = mat_ref.shape
    PW = pan_ref.shape[2]
    row = lax.axis_index("row")
    z = lax.axis_index("col")
    inv = inverse(g_ref[...])
    half = k_ref[...]
    proj = half + half.T
    t_rows = pan_ref[...].reshape(NZ * TR, PW)
    w_rows = wr_ref[...].reshape(NZ * TR, PW)
    left = dot_nn(t_rows, inv)
    right = dot_nn(w_rows - 2.0 * dot_nn(left, proj), inv)
    sub = lax.broadcasted_iota(jnp.int32, (TR, WIDTH), 0) + row * TR
    lane = lax.broadcasted_iota(jnp.int32, (TR, WIDTH), 1)
    change = dot_nt(left, wc_ref[...]) + dot_nt(right, tc_ref[...])
    change = change.reshape(NZ, TR, WIDTH)
    for a in range(NZ):
        new = mat_ref[a] - 2.0 * change[a]
        keep = jnp.logical_or(z < a, jnp.logical_and(z == a, sub >= lane))
        out_ref[a] = jnp.where(keep, new, 0.0)


def finish(matrix, panel, gram, proj, t_cols, w_cols, w_rows):
    vmem = pl.BlockSpec(memory_space=pltpu.VMEM)
    return pl.pallas_call(
        finish_kernel,
        out_shape=jax.ShapeDtypeStruct(matrix.shape, jnp.float32),
        in_specs=[vmem] * 7,
        out_specs=vmem,
        compiler_params=pltpu.CompilerParams(vmem_limit_bytes=32 * 2**20),
        name="finish",
    )(matrix, panel, gram, proj, t_cols, w_cols, w_rows)


def per_device(matrix, panel):
    NZ, _, TR, WIDTH = matrix.shape
    PW = panel.shape[3]
    NX, NY = PLANES[lax.axis_size("row")]
    sizes = (NX, NY, NZ, TR, WIDTH, PW)
    mat = matrix.reshape(NZ, TR, WIDTH)
    pan = panel.reshape(NZ, TR, PW)
    gram, proj, t_cols, w_cols, w_rows = exchange(mat, pan, sizes)
    out = finish(mat, pan, gram.reshape(PW, PW), proj.reshape(PW, PW),
                 t_cols.reshape(WIDTH, PW), w_cols.reshape(WIDTH, PW), w_rows)
    return out.reshape(NZ, 1, TR, WIDTH)


def solution(mesh):
    in_specs = (P(None, "row", None, "col"), P(None, "row", None, None))
    out_specs = P(None, "row", None, "col")
    return jax.shard_map(
        per_device, mesh=mesh, in_specs=in_specs, out_specs=out_specs, check_vma=False)
```

time: 717 us -> 129 us (0.18); the launches traced: 706 us -> 128 us
  waiting for transfers between devices: 481 us -> 0 us
  Pallas kernels: 0 us -> 126 us
  other arithmetic: 105 us -> 0 us
  local copies, waits for them, and re-layouts: 47.1 us -> 2.09 us
  matrix products: 31.2 us -> 0 us
  starting transfers between devices: 26.3 us -> 0 us
  between operations: 15.7 us -> 0.01 us
    psum x2 -> x0, waiting for transfers between devices: 282 us -> none  [the longest x1 178 us: per_device(): gram = lax.psum(transposed_product(panel_rows, panel_rows), 'row')]
    all_gather x3 -> x0, waiting for transfers between devices: 176 us -> none  [the longest x2 118 us: across_rows(): gathered = lax.all_gather(own_part[:, None], 'row', axis=1, tiled=True)]
    pallas_call x0 -> x2, Pallas kernels: none -> 126 us  [the longest x1 96.2 us: exchange(): pl.pallas_call(functools.partial(comm_kernel, sizes), out_shape=[shape(NZ...]
    another operation x13 -> x0, other arithmetic: 87 us -> none  [the longest x10 56.6 us: factor_inverse(): lower_factor = jnp.linalg.cholesky(gram)]
    all_to_all x2 -> x0, starting transfers between devices: 25.5 us -> none  [the longest x1 15.7 us: per_device(): lax.all_to_all(by_block, 'col', split_axis=0, concat_axis=0, tiled=True)]
    all_to_all x2 -> x0, waiting for transfers between devices: 23.2 us -> none  [the longest x1 23.2 us: per_device(): lax.all_to_all(strips, 'row', split_axis=4, concat_axis=4, tiled=True)]
    dot_general x9 -> x0, matrix products: 23.2 us -> none  [the longest x3 7.89 us: plain_product(): jnp.dot(left, right, precision=exact_mode, preferred_element_type=jnp.flo...]
    all_to_all x3 -> x0, local copies, waits for them, and re-layouts: 12.9 us -> none  [the longest x2 6.62 us: per_device(): lax.all_to_all(by_block, 'col', split_axis=0, concat_axis=0, tiled=True)]
  transfers between devices with their start and end apart: 7 -> 0, of which waited for: 6 -> 0; matrix products, arithmetic and copies ran while one was open for 22% -> 0% of each run, Pallas kernels for 0% -> 0%
where the time goes in v1:
time: 129 us; the launch traced here: 128 us
  Pallas kernels  126 us (98%)
  local copies, waits for them, and re-layouts  2.09 us (2%)
    pallas_call x1, Pallas kernels, exchange(): pl.pallas_call(functools.partial(comm_kernel, sizes), out_shape=[shape(NZ...  96.2 us
    pallas_call x1, Pallas kernels, finish(): pl.pallas_call(finish_kernel, out_shape=jax.ShapeDtypeStruct(matrix.shape...  29.5 us

profile of v1, /device:TPU:1, one launch (start us, length us, event | category | flops | bytes accessed | tf_op | source)
XLA Modules:
  0.0 127.8 jit_solution(8864715352616398102)
XLA Ops:
  0.0 0.0 copy-start
  0.0 1.1 copy-done
  1.1 0.0 copy-start.1
  1.1 1.0 copy-done.1
  2.1 96.2 %exchange.1 = (f32[12,2,16,384]{3,2,1,0:T(8,128)S(1)}, f32[2,4,6,8,384]{4,3,2,1,0:T(8,128)S(1)}, f32[4,8,2,16,384]{4,3,2,1,0:T(8,128)S(1)}, f32[4,8,2,16,384]{4,3,2,1,0:T(8,128)S(1)}, f32[12,16,384]{2,1,0:T(8,128)S(1)}) custom-call(f32[12,16,1024]{2,1,0:T(8,128)S(1)} %bitcast.9, f32[12,16,384]{2,1,0:T(8,128)S(1)} %bitcast.13), custom_call_target="tpu_custom_call" | custom-call | tf_op jit(solution)/shard_map/exchange/pallas_call | solution.py:304
  98.3 29.5 %finish.1 = f32[12,16,1024]{2,1,0:T(8,128)} custom-call(f32[12,16,1024]{2,1,0:T(8,128)S(1)} %bitcast.10, f32[12,16,384]{2,1,0:T(8,128)S(1)} %bitcast.14, f32[384,384]{1,0:T(8,128)S(1)} %bitcast.15, f32[384,384]{1,0:T(8,128)S(1)} %bitcast.16, f32[1024,384]{1,0:T(8,128)S(1)} %bitcast.11, f32[1024,384]{1,0:T(8,128)S(1)} %bitcast.12, ...), custom_call_target="tpu_custom_call" | custom-call | tf_op jit(solution)/shard_map/finish/pallas_call | solution.py:375
Async XLA Ops:
  0.0 1.1 copy-start
  1.1 1.0 copy-start.1

commit v2 on v1

v2 whole, which is shorter than its diff:
```python
import functools

import jax
import jax.numpy as jnp
from jax import lax
from jax.experimental import pallas as pl
from jax.experimental.pallas import tpu as pltpu
from jax.sharding import PartitionSpec as P

EXACT = lax.Precision.HIGHEST
PLANES = {64: (4, 8), 8: (2, 2)}


def dot_nn(a, b):
    return lax.dot_general(a, b, (((1,), (0,)), ((), ())), precision=EXACT,
                           preferred_element_type=jnp.float32)


def dot_tn(a, b):
    return lax.dot_general(a, b, (((0,), (0,)), ((), ())), precision=EXACT,
                           preferred_element_type=jnp.float32)


def dot_nt(a, b):
    return lax.dot_general(a, b, (((1,), (1,)), ((), ())), precision=EXACT,
                           preferred_element_type=jnp.float32)


def two_parts(a):
    high = a.astype(jnp.bfloat16)
    return high, (a - high.astype(jnp.float32)).astype(jnp.bfloat16)


def dot_split(a, b, dims):
    ah, al = two_parts(a)
    bh, bl = two_parts(b)
    dot = lambda p, q: lax.dot_general(p, q, (dims, ((), ())), preferred_element_type=jnp.float32)
    return dot(ah, bh) + (dot(ah, bl) + dot(al, bh))


NN, TN, NT = ((1,), (0,)), ((0,), (0,)), ((1,), (1,))


def by_distance(n):
    return sorted(range(1, n), key=lambda d: (min(d, n - d), d))


def scaled_gram(gram):
    n = gram.shape[0]
    eye = jnp.where(lax.broadcasted_iota(jnp.int32, (n, n), 0)
                    == lax.broadcasted_iota(jnp.int32, (n, n), 1), 1.0, 0.0)
    diag = gram * eye
    s_row = lax.rsqrt(jnp.sum(diag, axis=0, keepdims=True))
    s_col = lax.rsqrt(jnp.sum(diag, axis=1, keepdims=True))
    scaled = gram * s_row * s_col
    bound = jnp.max(jnp.sum(jnp.abs(scaled), axis=0, keepdims=True))
    return scaled, eye, s_row, s_col, eye * (2.0 / (1.0 + bound))


FIXED_STEPS = 7


def comm_kernel(sizes, mat_hbm, pan_hbm, g_ref, k_ref, tc_ref, wc_ref, wr_ref, inv_ref, err_ref,
                mat_ref, pan_ref, sg_ref,
                h_ref, gl_ref, gc_ref, gsum_ref, gx_ref, gsx_ref, gy_ref, gf_ref,
                mp_ref, cx_ref, mx_ref, ms_ref, my_ref,
                dp_ref, rz_ref, kp_ref, kc_ref, kx_ref, ks_ref, ky_ref, kz_ref, kf_ref,
                in_sems,
                send_sems, t_sems, w_sems, wz_sems, mc_sems, mx_sems, my_sems, dz_sems,
                g_sems, gz_sems, k_sems, kz_sems, ka_sems):
    NX, NY, NZ, TR, WIDTH, PW = sizes
    TS = NX * NY * 2
    NP = PW // 2 // NX // 8
    row = lax.axis_index("row")
    z = lax.axis_index("col")
    core = lax.rem(row, 2)
    chip = lax.div(row, 2)
    y = lax.rem(chip, NY)
    x = lax.div(chip, NY)
    other = 1 - core

    def at(x_, y_, c_):
        return (x_ * NY + y_) * 2 + c_

    def xp(d):
        return lax.rem(x + d, NX)

    def yp(d):
        return lax.rem(y + d, NY)

    def zp(d):
        return lax.rem(z + d, NZ)

    to_x = lambda d: (at(xp(d), y, core), z)
    to_y = lambda d: (at(x, yp(d), core), z)
    to_z = lambda d: (row, zp(d))
    to_core = (at(x, y, other), z)

    barrier = pltpu.get_barrier_semaphore()
    peers = ([to_x(d) for d in range(1, NX)] + [to_y(d) for d in range(1, NY)]
             + [to_z(d) for d in range(1, NZ)] + [to_core])
    for peer in peers:
        pl.semaphore_signal(barrier, inc=1, device_id=peer, device_id_type=pl.DeviceIdType.MESH)

    pan_in = pltpu.make_async_copy(pan_hbm, pan_ref, in_sems.at[0])
    mat_in = pltpu.make_async_copy(mat_hbm, mat_ref, in_sems.at[1])
    pan_in.start()
    mat_in.start()

    sent = []

    def send(src, dst, sem, peer, when=None):
        slot = len(sent)
        sent.append((src, when))
        pltpu.make_async_remote_copy(
            src_ref=src, dst_ref=dst, send_sem=send_sems.at[slot], recv_sem=sem,
            device_id=peer, device_id_type=pl.DeviceIdType.MESH).start()

    def left(slot, src):
        pltpu.make_async_remote_copy(
            src_ref=src, dst_ref=src, send_sem=send_sems.at[slot], recv_sem=t_sems.at[0],
            device_id=to_core, device_id_type=pl.DeviceIdType.MESH).wait_send()

    def arrive(dst, sem):
        pltpu.make_async_remote_copy(
            src_ref=dst, dst_ref=dst, send_sem=send_sems.at[0], recv_sem=sem,
            device_id=to_core, device_id_type=pl.DeviceIdType.MESH).wait_recv()

    YD, XD, ZD = by_distance(NY), by_distance(NX), by_distance(NZ)

    pan_in.wait()
    tc_ref[x, y, core] = pan_ref[z]
    t_rows = pan_ref[...].reshape(NZ * TR, PW)
    gl_ref[...] = dot_tn(t_rows, t_rows).reshape(NZ, 2, PW // NZ // 2, PW)
    mat_in.wait()
    sub = lax.broadcasted_iota(jnp.int32, (TR, WIDTH), 0) + row * TR
    lane = lax.broadcasted_iota(jnp.int32, (TR, WIDTH), 1)
    for a in range(NZ):
        tile = mat_ref[a]
        diag_part = jnp.where(sub > lane, tile, jnp.where(sub == lane, 0.5 * tile, 0.0))
        h_ref[a] = jnp.where(z < a, tile, jnp.where(z == a, diag_part, 0.0))
    XW = WIDTH // NX
    for d in list(XD) + [0]:
        xb = xp(d)
        cols = pl.ds(pl.multiple_of(xb * XW, XW), XW)
        h = h_ref[:, :, cols].reshape(NZ * TR, XW)
        mp_ref[xb] = dot_tn(h, t_rows).reshape(NY, 2, TR, PW)
    pl.semaphore_wait(barrier, len(peers))

    own_t = pan_ref.at[z]
    for d in YD:
        send(own_t, tc_ref.at[x, y, core], t_sems.at[row], to_y(d))
    for d in XD:
        send(own_t, tc_ref.at[x, y, core], t_sems.at[row], to_x(d))
    send(gl_ref.at[z, other], gc_ref, g_sems.at[0], to_core)
    for d in list(XD) + [0]:
        send(mp_ref.at[xp(d), :, other], cx_ref.at[xp(d)], mc_sems.at[xp(d)], to_core)

    arrive(gc_ref, g_sems.at[0])
    gsum_ref[...] = gl_ref[z, core] + gc_ref[...]
    for d in XD:
        send(gsum_ref, gx_ref.at[d - 1], g_sems.at[d], to_x(d))

    for d in YD:
        tile = tc_ref.at[x, yp(NY - d), core]
        sem = t_sems.at[at(x, yp(NY - d), core)]
        arrive(tile, sem)
        for dx in XD:
            send(tile, tile, sem, to_x(dx))
    send(tc_ref.at[x, :, core], tc_ref.at[x, :, core], t_sems.at[TS + x], to_core)

    gs = gsum_ref[...]
    for d in XD:
        arrive(gx_ref.at[d - 1], g_sems.at[d])
        gs = gs + gx_ref[d - 1]
    gsx_ref[...] = gs
    for d in YD:
        send(gsx_ref, gy_ref.at[d - 1], g_sems.at[NX + d], to_y(d))

    for d in list(XD) + [0]:
        xb = xp(d)
        arrive(cx_ref.at[xb], mc_sems.at[xb])
        ms_ref[xb] = mp_ref[xb, :, core] + cx_ref[xb]
        if d:
            send(ms_ref.at[xb], mx_ref.at[d - 1], mx_sems.at[d - 1], to_x(d))

    for dx in XD:
        xb = xp(NX - dx)
        for dy in [0] + YD:
            arrive(tc_ref.at[xb, yp(NY - dy), core], t_sems.at[at(xb, yp(NY - dy), core)])
        send(tc_ref.at[xb, :, core], tc_ref.at[xb, :, core], t_sems.at[TS + xb], to_core)

    gs = gsx_ref[...]
    for d in YD:
        arrive(gy_ref.at[d - 1], g_sems.at[NX + d])
        gs = gs + gy_ref[d - 1]
    gf_ref[...] = gs
    g_ref[z, core] = gs
    for d in ZD:
        send(gf_ref, g_ref.at[z, core], gz_sems.at[d - 1], to_z(d))

    for dx in [0] + XD:
        xb = xp(NX - dx)
        arrive(tc_ref.at[xb, :, other], t_sems.at[TS + xb])

    direct = dot_split(h_ref[...].reshape(NZ * TR, WIDTH), tc_ref[...].reshape(WIDTH, PW), NN)
    dp_ref[...] = direct.reshape(NZ, TR, PW)
    for d in ZD:
        send(dp_ref.at[zp(d)], rz_ref.at[d - 1], dz_sems.at[d - 1], to_z(d))
    kp_ref[...] = dot_split(t_rows, direct, TN).reshape(2, NX, NP, 8, PW)
    send(kp_ref.at[other], kc_ref, k_sems.at[0], to_core)

    msum = ms_ref[x]
    for d in XD:
        arrive(mx_ref.at[d - 1], mx_sems.at[d - 1])
        msum = msum + mx_ref[d - 1]
    mp_ref[x, :, core] = msum
    for d in YD:
        send(mp_ref.at[x, yp(d), core], my_ref.at[d - 1], my_sems.at[d - 1], to_y(d))

    arrive(kc_ref, k_sems.at[0])
    ks_ref[...] = kp_ref[core] + kc_ref[...]
    for d in XD:
        send(ks_ref.at[xp(d)], kx_ref.at[d - 1], k_sems.at[d], to_x(d))

    msum = mp_ref[x, y, core]
    for d in YD:
        arrive(my_ref.at[d - 1], my_sems.at[d - 1])
        msum = msum + my_ref[d - 1]

    for d in ZD:
        arrive(g_ref.at[zp(NZ - d), core], gz_sems.at[d - 1])
    send(g_ref.at[:, core], g_ref.at[:, core], g_sems.at[NX + NY], to_core)

    ksum = ks_ref[x]
    for d in XD:
        arrive(kx_ref.at[d - 1], k_sems.at[d])
        ksum = ksum + kx_ref[d - 1]
    ks_ref[x] = ksum
    for d in YD:
        piece = ks_ref.at[x, lax.min(yp(d), NP - 1)]
        goes = yp(d) < NP

        @pl.when(goes)
        def _():
            send(piece, ky_ref.at[d - 1], k_sems.at[NX + d], to_y(d), goes)

    wsum = msum + dp_ref[z]
    for d in ZD:
        arrive(rz_ref.at[d - 1], dz_sems.at[d - 1])
        wsum = wsum + rz_ref[d - 1]
    wc_ref[x, y, core] = wsum
    wr_ref[z] = wsum
    for d in YD:
        send(wc_ref.at[x, y, core], wc_ref.at[x, y, core], w_sems.at[row], to_y(d))
    for d in XD:
        send(wc_ref.at[x, y, core], wc_ref.at[x, y, core], w_sems.at[row], to_x(d))

    held = y < NP
    yy = lax.min(y, NP - 1)

    @pl.when(held)
    def _():
        ksum = ks_ref[x, yy]
        for d in YD:
            arrive(ky_ref.at[d - 1], k_sems.at[NX + d])
            ksum = ksum + ky_ref[d - 1]
        kf_ref[...] = ksum
        for d in ZD:
            send(kf_ref, kz_ref.at[d - 1], kz_sems.at[d - 1], to_z(d), held)

    for d in ZD:
        send(wr_ref.at[z], wr_ref.at[z], wz_sems.at[d - 1], to_z(d))

    arrive(g_ref.at[:, other], g_sems.at[NX + NY])
    scaled, eye, s_row, s_col, start = scaled_gram(g_ref[...].reshape(PW, PW))
    sg_ref[...] = scaled
    inv_ref[...] = start

    def newton(count):
        for _ in range(count):
            residual = eye - dot_split(sg_ref[...], inv_ref[...], NN)
            inv_ref[...] += dot_split(inv_ref[...], residual, NN)

    newton(1)

    for d in YD:
        tile = wc_ref.at[x, yp(NY - d), core]
        sem = w_sems.at[at(x, yp(NY - d), core)]
        arrive(tile, sem)
        for dx in XD:
            send(tile, tile, sem, to_x(dx))
    send(wc_ref.at[x, :, core], wc_ref.at[x, :, core], w_sems.at[TS + x], to_core)
    newton(2)

    own_k = k_ref.at[core, x, yy]

    @pl.when(held)
    def _():
        ksum = kf_ref[...]
        for d in ZD:
            arrive(kz_ref.at[d - 1], kz_sems.at[d - 1])
            ksum = ksum + kz_ref[d - 1]
        k_ref[core, x, yy] = ksum
        for d in YD:
            send(own_k, own_k, ka_sems.at[d], to_y(d), held)

    for dx in XD:
        xb = xp(NX - dx)
        for dy in [0] + YD:
            arrive(wc_ref.at[xb, yp(NY - dy), core], w_sems.at[at(xb, yp(NY - dy), core)])
        send(wc_ref.at[xb, :, core], wc_ref.at[xb, :, core], w_sems.at[TS + xb], to_core)
    newton(2)

    for d in YD:
        src_y = yp(NY - d)

        @pl.when(src_y < NP)
        def _():
            piece = k_ref.at[core, x, lax.min(src_y, NP - 1)]
            arrive(piece, ka_sems.at[d])
    for d in XD:
        send(k_ref.at[core, x], k_ref.at[core, x], ka_sems.at[NY + d], to_x(d))
    newton(FIXED_STEPS - 5)
    for d in XD:
        arrive(k_ref.at[core, xp(NX - d)], ka_sems.at[NY + d])
    send(k_ref.at[core], k_ref.at[core], ka_sems.at[0], to_core)

    residual = eye - dot_nn(sg_ref[...], inv_ref[...])
    err_ref[...] = jnp.full(err_ref.shape, jnp.sum(residual * residual), jnp.float32)
    inv_ref[...] += dot_split(inv_ref[...], residual, NN)

    for d in ZD:
        arrive(wr_ref.at[zp(NZ - d)], wz_sems.at[d - 1])
    for dx in [0] + XD:
        xb = xp(NX - dx)
        arrive(wc_ref.at[xb, :, other], w_sems.at[TS + xb])
    arrive(k_ref.at[other], ka_sems.at[0])
    for slot, (src, when) in enumerate(sent):
        if when is None:
            left(slot, src)
        else:
            pl.when(when)(functools.partial(left, slot, src))


def exchange(matrix, panel, sizes):
    NX, NY, NZ, TR, WIDTH, PW = sizes
    f32 = jnp.float32
    TS = NX * NY * 2
    NP = PW // 2 // NX // 8
    GR = PW // NZ // 2
    vmem = pl.BlockSpec(memory_space=pltpu.VMEM)
    shape = lambda *s: jax.ShapeDtypeStruct(s, f32)
    V = lambda *s: pltpu.VMEM(s, f32)
    D = lambda n: pltpu.SemaphoreType.DMA((n,))
    return pl.pallas_call(
        functools.partial(comm_kernel, sizes),
        out_shape=[shape(NZ, 2, GR, PW), shape(2, NX, NP, 8, PW), shape(NX, NY, 2, TR, PW),
                   shape(NX, NY, 2, TR, PW), shape(NZ, TR, PW), shape(PW, PW), shape(8, 128)],
        in_specs=[pl.BlockSpec(memory_space=pl.ANY)] * 2,
        out_specs=[vmem] * 7,
        scratch_shapes=[
            V(NZ, TR, WIDTH), V(NZ, TR, PW), V(PW, PW),
            V(NZ, TR, WIDTH), V(NZ, 2, GR, PW), V(GR, PW), V(GR, PW), V(NX - 1, GR, PW), V(GR, PW),
            V(NY - 1, GR, PW), V(GR, PW),
            V(NX, NY, 2, TR, PW), V(NX, NY, TR, PW), V(NX - 1, NY, TR, PW), V(NX, NY, TR, PW),
            V(NY - 1, TR, PW),
            V(NZ, TR, PW), V(NZ - 1, TR, PW), V(2, NX, NP, 8, PW), V(NX, NP, 8, PW),
            V(NX - 1, NP, 8, PW), V(NX, NP, 8, PW), V(NY - 1, 8, PW), V(NZ - 1, 8, PW), V(8, PW),
            D(2), D(200), D(TS + NX), D(TS + NX), D(NZ - 1), D(NX), D(NX - 1), D(NY - 1), D(NZ - 1),
            D(NX + NY + 1), D(NZ - 1), D(NX + NY), D(NZ - 1), D(NX + NY),
        ],
        compiler_params=pltpu.CompilerParams(
            collective_id=0, has_side_effects=True, vmem_limit_bytes=32 * 2**20),
        name="exchange",
    )(matrix, panel)


def polish(gram, guess, error):
    scaled, eye, s_row, s_col, start = scaled_gram(gram)
    usable = error < 0.25

    def step(state):
        count, _, guess = state
        residual = eye - dot_nn(scaled, guess)
        error = jnp.sum(residual * residual)
        return count + 1, error, guess + dot_nn(guess, residual)

    def again(state):
        return jnp.logical_and(state[1] > 1e-8, state[0] < 80)

    state = (0, jnp.where(usable, error, 1.0), jnp.where(usable, guess, start))
    _, _, found = lax.while_loop(again, step, state)
    return found * s_row * s_col


def finish_kernel(mat_ref, pan_ref, g_ref, k_ref, tc_ref, wc_ref, wr_ref, inv_ref, err_ref, out_ref):
    NZ, TR, WIDTH = mat_ref.shape
    PW = pan_ref.shape[2]
    row = lax.axis_index("row")
    z = lax.axis_index("col")
    inv = polish(g_ref[...], inv_ref[...], err_ref[0, 0])
    half = k_ref[...]
    proj = half + half.T
    t_rows = pan_ref[...].reshape(NZ * TR, PW)
    w_rows = wr_ref[...].reshape(NZ * TR, PW)
    left = dot_nn(t_rows, inv)
    right = dot_nn(w_rows - 2.0 * dot_nn(left, proj), inv)
    sub = lax.broadcasted_iota(jnp.int32, (TR, WIDTH), 0) + row * TR
    lane = lax.broadcasted_iota(jnp.int32, (TR, WIDTH), 1)
    change = dot_split(left, wc_ref[...], NT) + dot_split(right, tc_ref[...], NT)
    change = change.reshape(NZ, TR, WIDTH)
    for a in range(NZ):
        new = mat_ref[a] - 2.0 * change[a]
        keep = jnp.logical_or(z < a, jnp.logical_and(z == a, sub >= lane))
        out_ref[a] = jnp.where(keep, new, 0.0)


def finish(*operands):
    matrix = operands[0]
    vmem = pl.BlockSpec(memory_space=pltpu.VMEM)
    return pl.pallas_call(
        finish_kernel,
        out_shape=jax.ShapeDtypeStruct(matrix.shape, jnp.float32),
        in_specs=[vmem] * len(operands),
        out_specs=vmem,
        compiler_params=pltpu.CompilerParams(vmem_limit_bytes=32 * 2**20),
        name="finish",
    )(*operands)


def per_device(matrix, panel):
    NZ, _, TR, WIDTH = matrix.shape
    PW = panel.shape[3]
    NX, NY = PLANES[lax.axis_size("row")]
    sizes = (NX, NY, NZ, TR, WIDTH, PW)
    mat = matrix.reshape(NZ, TR, WIDTH)
    pan = panel.reshape(NZ, TR, PW)
    gram, proj, t_cols, w_cols, w_rows, guess, error = exchange(mat, pan, sizes)
    out = finish(mat, pan, gram.reshape(PW, PW), proj.reshape(PW, PW),
                 t_cols.reshape(WIDTH, PW), w_cols.reshape(WIDTH, PW), w_rows, guess, error)
    return out.reshape(NZ, 1, TR, WIDTH)


def solution(mesh):
    in_specs = (P(None, "row", None, "col"), P(None, "row", None, None))
    out_specs = P(None, "row", None, "col")
    return jax.shard_map(
        per_device, mesh=mesh, in_specs=in_specs, out_specs=out_specs, check_vma=False)
```

time: 129 us -> 91.3 us (0.71)
  Pallas kernels: 126 us -> 89 us
    pallas_call x1, Pallas kernels: 29.5 us -> 5.29 us  [finish(): pl.pallas_call(finish_kernel, out_shape=jax.ShapeDtypeStruct(matrix.shape...]
    pallas_call x1, Pallas kernels: 96.2 us -> 83.7 us  [exchange(): pl.pallas_call(functools.partial(comm_kernel, sizes), out_shape=[shape(NZ...]
where the time goes in v2:
time: 91.3 us; the launch traced here: 91.1 us
  Pallas kernels  89 us (97%)
  local copies, waits for them, and re-layouts  2.09 us (2%)
    pallas_call x1, Pallas kernels, exchange(): pl.pallas_call(functools.partial(comm_kernel, sizes), out_shape=[shape(NZ...  83.7 us
    pallas_call x1, Pallas kernels, finish(): pl.pallas_call(finish_kernel, out_shape=jax.ShapeDtypeStruct(matrix.shape...  5.29 us
    unnamed x4, local copies, waits for them, and re-layouts  2.09 us

profile of v2, /device:TPU:1, one launch (start us, length us, event | category | flops | bytes accessed | tf_op | source)
XLA Modules:
  0.0 91.1 jit_solution(524230453914918659)
XLA Ops:
  0.0 0.0 copy-start
  0.0 1.1 %copy-done = f32[12,1,16,1024]{3,2,1,0:T(8,128)S(1)} copy-done((f32[12,1,16,1024]{3,2,1,0:T(8,128)S(1)}, f32[12,1,16,1024]{3,2,1,0:T(8,128)}, u32[]{:S(2)}) %copy-start) | copy-done | bytes 786456
  1.1 0.0 copy-start.1
  1.1 1.0 %copy-done.1 = f32[12,1,16,384]{3,2,1,0:T(8,128)S(1)} copy-done((f32[12,1,16,384]{3,2,1,0:T(8,128)S(1)}, f32[12,1,16,384]{3,2,1,0:T(8,128)}, u32[]{:S(2)}) %copy-start.1) | copy-done | bytes 294936
  2.1 83.7 %exchange.1 = (f32[12,2,16,384]{3,2,1,0:T(8,128)S(1)}, f32[2,4,6,8,384]{4,3,2,1,0:T(8,128)S(1)}, f32[4,8,2,16,384]{4,3,2,1,0:T(8,128)S(1)}, f32[4,8,2,16,384]{4,...) custom-call(f32[12,16,1024]{2,1,0:T(8,128)S(1)} %bitcast.9, ...), custom_call_target="tpu_custom_call" | custom-call | tf_op jit(solution)/shard_map/exchange/pallas_call | solution.py:356
  85.8 5.3 %finish.1 = f32[12,16,1024]{2,1,0:T(8,128)} custom-call(f32[12,16,1024]{2,1,0:T(8,128)S(1)} %bitcast.10, f32[12,16,384]{2,1,0:T(8,128)S(1)} %bitcast.14, f32[384,384]{1,0:T(8,128)S(1)} %bitcast.15, f32[384,384]{1,0:T(8,128)S(1)} %bitcast.16, f32[1024,384]{1,0:T(8,128)S(1)} %bitcast.11, f32[1024,384]{1,0:T(8,128)S(1)} %bitcast.12, ...), custom_call_target="tpu_custom_call" | custom-call | tf_op jit(solution)/shard_map/finish/pallas_call | solution.py:422
Async XLA Ops:
  0.0 1.1 %copy-start = (f32[12,1,16,1024]{3,2,1,0:T(8,128)S(1)}, f32[12,1,16,1024]{3,2,1,0:T(8,128)}, u32[]{:S(2)}) copy-start(f32[12,1,16,1024]{3,2,1,0:T(8,128)} %param.2) | copy-start | bytes 2359300
  1.1 1.0 %copy-start.1 = (f32[12,1,16,384]{3,2,1,0:T(8,128)S(1)}, f32[12,1,16,384]{3,2,1,0:T(8,128)}, u32[]{:S(2)}) copy-start(f32[12,1,16,384]{3,2,1,0:T(8,128)} %param.3) | copy-start | bytes 884740

commit v3 on v2

v3 whole, which is shorter than its diff:
```python
import functools

import jax
import jax.numpy as jnp
from jax import lax
from jax.experimental import pallas as pl
from jax.experimental.pallas import tpu as pltpu
from jax.sharding import PartitionSpec as P

EXACT = lax.Precision.HIGHEST
PLANES = {64: (4, 8), 8: (2, 2)}


def dot_nn(a, b):
    return lax.dot_general(a, b, (((1,), (0,)), ((), ())), precision=EXACT,
                           preferred_element_type=jnp.float32)


def dot_tn(a, b):
    return lax.dot_general(a, b, (((0,), (0,)), ((), ())), precision=EXACT,
                           preferred_element_type=jnp.float32)


def dot_nt(a, b):
    return lax.dot_general(a, b, (((1,), (1,)), ((), ())), precision=EXACT,
                           preferred_element_type=jnp.float32)


def two_parts(a):
    high = a.astype(jnp.bfloat16)
    return high, (a - high.astype(jnp.float32)).astype(jnp.bfloat16)


def dot_split(a, b, dims):
    ah, al = two_parts(a)
    bh, bl = two_parts(b)
    dot = lambda p, q: lax.dot_general(p, q, (dims, ((), ())), preferred_element_type=jnp.float32)
    return dot(ah, bh) + (dot(ah, bl) + dot(al, bh))


NN, TN, NT = ((1,), (0,)), ((0,), (0,)), ((1,), (1,))


def by_distance(n):
    return sorted(range(1, n), key=lambda d: (min(d, n - d), d))


def scaled_gram(gram):
    n = gram.shape[0]
    eye = jnp.where(lax.broadcasted_iota(jnp.int32, (n, n), 0)
                    == lax.broadcasted_iota(jnp.int32, (n, n), 1), 1.0, 0.0)
    diag = gram * eye
    s_row = lax.rsqrt(jnp.sum(diag, axis=0, keepdims=True))
    s_col = lax.rsqrt(jnp.sum(diag, axis=1, keepdims=True))
    scaled = gram * s_row * s_col
    bound = jnp.max(jnp.sum(jnp.abs(scaled), axis=0, keepdims=True))
    return scaled, eye, s_row, s_col, eye * (2.0 / (1.0 + bound))


COARSE_STEPS = 4


def comm_kernel(sizes, mat_hbm, pan_hbm, g_ref, k_ref, tc_ref, wc_ref, wr_ref, inv_ref, err_ref,
                mat_ref, pan_ref, sg_ref, units_ref, h_ref,
                gl_ref, gc_ref, gsum_ref, gx_ref, gsx_ref, gy_ref,
                mpa_ref, mpb_ref, ca_ref, cb_ref, ax_ref, ay_ref, by_ref, bs_ref, bx_ref,
                dp_ref, rz_ref, kp_ref, kc_ref, kx_ref, ks_ref, ky_ref, kz_ref, kf_ref,
                in_sems, out_sems, ky_out_sems, t_sems, w_sems, wz_sems, ma_sems, mb_sems, dz_sems,
                g_sems, gz_sems, ga_sems, k_sems, kz_sems, ka_sems):
    NX, NY, NZ, TR, WIDTH, PW, NL, LA = sizes
    NP = PW // 2 // NX // 8
    LW = PW // NL
    row = lax.axis_index("row")
    z = lax.axis_index("col")
    core = lax.rem(row, 2)
    chip = lax.div(row, 2)
    y = lax.rem(chip, NY)
    x = lax.div(chip, NY)
    other = 1 - core

    def at(x_, y_, c_):
        return (x_ * NY + y_) * 2 + c_

    def xp(d):
        return lax.rem(x + d, NX)

    def yp(d):
        return lax.rem(y + d, NY)

    def zp(d):
        return lax.rem(z + d, NZ)

    to_x = lambda d: (at(xp(d), y, core), z)
    to_y = lambda d: (at(x, yp(d), core), z)
    to_z = lambda d: (row, zp(d))
    to_core = (at(x, y, other), z)

    barrier = pltpu.get_barrier_semaphore()
    peers = ([to_x(d) for d in range(1, NX)] + [to_y(d) for d in range(1, NY)]
             + [to_z(d) for d in range(1, NZ)] + [to_core])
    for peer in peers:
        pl.semaphore_signal(barrier, inc=1, device_id=peer, device_id_type=pl.DeviceIdType.MESH)

    pan_in = pltpu.make_async_copy(pan_hbm, pan_ref, in_sems.at[0])
    mat_in = pltpu.make_async_copy(mat_hbm, mat_ref, in_sems.at[1])
    pan_in.start()
    mat_in.start()

    totals = {}

    def send(src, dst, sem, peer, out):
        words = 1
        for n in src.shape:
            words *= n
        totals[out] = totals.get(out, 0) + words
        pltpu.make_async_remote_copy(
            src_ref=src, dst_ref=dst, send_sem=out_sems.at[out], recv_sem=sem,
            device_id=peer, device_id_type=pl.DeviceIdType.MESH).start()

    def left(ref, sem):
        pltpu.make_async_remote_copy(
            src_ref=ref, dst_ref=ref, send_sem=sem, recv_sem=t_sems.at[0],
            device_id=to_core, device_id_type=pl.DeviceIdType.MESH).wait_send()

    def all_left(out):
        assert totals[out] % (8 * PW) == 0
        left(units_ref.at[pl.ds(0, totals[out] // (8 * PW))], out_sems.at[out])

    def arrive(dst, sem):
        pltpu.make_async_remote_copy(
            src_ref=dst, dst_ref=dst, send_sem=out_sems.at[0], recv_sem=sem,
            device_id=to_core, device_id_type=pl.DeviceIdType.MESH).wait_recv()

    OUT_T, OUT_W, OUT_MA, OUT_MB, OUT_D, OUT_K, OUT_KZ, OUT_KY, OUT_G, OUT_GS, OUT_GX, OUT_GC = range(12)
    YD, XD, ZD = by_distance(NY), by_distance(NX), by_distance(NZ)

    pan_in.wait()
    tc_ref[x, y, core] = pan_ref[z]
    t_rows = pan_ref[...].reshape(NZ * TR, PW)
    gram = dot_tn(t_rows, t_rows)
    for l in range(NL):
        gl_ref[l] = gram[:, l * LW:(l + 1) * LW].reshape(NZ, 2, PW // NZ // 2, LW)
    mat_in.wait()
    sub = lax.broadcasted_iota(jnp.int32, (TR, WIDTH), 0) + row * TR
    lane = lax.broadcasted_iota(jnp.int32, (TR, WIDTH), 1)
    for a in range(NZ):
        tile = mat_ref[a]
        diag_part = jnp.where(sub > lane, tile, jnp.where(sub == lane, 0.5 * tile, 0.0))
        h_ref[a] = jnp.where(z < a, tile, jnp.where(z == a, diag_part, 0.0))
    XW = WIDTH // NX

    def columns(xb):
        return h_ref[:, :, pl.ds(pl.multiple_of(xb * XW, XW), XW)].reshape(NZ * TR, XW)

    for d in [0] + XD:
        xb = xp(d)
        terms = dot_tn(columns(xb), t_rows).reshape(NY, 2, TR, PW)
        for c in range(2):
            mpa_ref[c, xb] = terms[:, c, :, :LA]
            mpb_ref[c, :, xb] = terms[:, c, :, LA:]
    pl.semaphore_wait(barrier, len(peers))

    own_t = pan_ref.at[z]
    for d in YD:
        send(own_t, tc_ref.at[x, y, core], t_sems.at[d], to_y(d), OUT_T)
    for d in XD:
        send(own_t, tc_ref.at[x, y, core], t_sems.at[NY + d], to_x(d), OUT_T)
    send(gl_ref.at[:, z, other], gc_ref, g_sems.at[0], to_core, OUT_G)
    send(mpb_ref.at[other], cb_ref, mb_sems.at[0], to_core, OUT_MB)
    send(mpa_ref.at[other], ca_ref, ma_sems.at[0], to_core, OUT_MA)

    holds_g = x < NL
    own_l = lax.min(x, NL - 1)
    arrive(gc_ref, g_sems.at[0])
    gsum_ref[...] = gl_ref[:, z, core] + gc_ref[...]
    for d in XD:
        @pl.when(xp(d) < NL)
        def _():
            pltpu.make_async_remote_copy(
                src_ref=gsum_ref.at[lax.min(xp(d), NL - 1)], dst_ref=gx_ref.at[d - 1],
                send_sem=ky_out_sems.at[NY + d], recv_sem=g_sems.at[d],
                device_id=to_x(d), device_id_type=pl.DeviceIdType.MESH).start()

    def forward_t(ds):
        for d in ds:
            tile = tc_ref.at[x, yp(NY - d), core]
            arrive(tile, t_sems.at[d])
            for dx in XD:
                send(tile, tile, t_sems.at[NY + dx], to_x(dx), OUT_T)

    forward_t(YD[:3])

    @pl.when(holds_g)
    def _():
        gs = gsum_ref[own_l]
        for d in XD:
            arrive(gx_ref.at[d - 1], g_sems.at[d])
            gs = gs + gx_ref[d - 1]
        gsx_ref[...] = gs
        for d in YD:
            send(gsx_ref, gy_ref.at[d - 1], g_sems.at[NX + d], to_y(d), OUT_GS)

    arrive(cb_ref, mb_sems.at[0])
    mpb_ref[core] = mpb_ref[core] + cb_ref[...]
    for d in YD:
        send(mpb_ref.at[core, yp(d)], by_ref.at[d - 1], mb_sems.at[d], to_y(d), OUT_MB)

    forward_t(YD[3:])
    send(tc_ref.at[x, :, core], tc_ref.at[x, :, core], t_sems.at[NY + NX], to_core, OUT_T)
    arrive(ca_ref, ma_sems.at[0])
    mpa_ref[core] = mpa_ref[core] + ca_ref[...]

    def project(xb):
        tiles = tc_ref[xb, :, core].reshape(NY * TR, PW)
        return (dot_split(tiles, mpa_ref[core, xb].reshape(NY * TR, LA), TN),
                dot_split(tiles, mpb_ref[core, :, xb].reshape(NY * TR, PW - LA), TN))

    ka, kb = project(x)
    for dx in XD:
        xb = xp(NX - dx)
        arrive(tc_ref.at[xb, :, core], t_sems.at[NY + dx])
        send(tc_ref.at[xb, :, core], tc_ref.at[xb, :, core], t_sems.at[NY + NX + dx], to_core, OUT_T)
        more_a, more_b = project(xb)
        ka, kb = ka + more_a, kb + more_b
        if dx == XD[min(1, len(XD) - 1)]:
            @pl.when(holds_g)
            def _():
                gs = gsx_ref[...]
                for d in YD:
                    arrive(gy_ref.at[d - 1], g_sems.at[NX + d])
                    gs = gs + gy_ref[d - 1]
                g_ref[own_l, z, core] = gs
                own_g = g_ref.at[own_l, z, core]
                for d in ZD:
                    send(own_g, own_g, gz_sems.at[d - 1], to_z(d), OUT_GS)
    kp_ref[:, :, :, :, :LA] = ka.reshape(2, NX, NP, 8, LA)
    kp_ref[:, :, :, :, LA:] = kb.reshape(2, NX, NP, 8, PW - LA)
    send(kp_ref.at[other], kc_ref, k_sems.at[0], to_core, OUT_K)

    arrive(tc_ref.at[x, :, other], t_sems.at[NY + NX])
    direct = dot_split(columns(x), tc_ref[x].reshape(XW, PW), NN)

    arrive(kc_ref, k_sems.at[0])
    ks_ref[...] = kp_ref[core] + kc_ref[...]
    for d in XD:
        send(ks_ref.at[xp(d)], kx_ref.at[d - 1], k_sems.at[d], to_x(d), OUT_K)

    for dx in XD:
        xb = xp(NX - dx)
        arrive(tc_ref.at[xb, :, other], t_sems.at[NY + NX + dx])
        direct = direct + dot_split(columns(xb), tc_ref[xb].reshape(XW, PW), NN)
    dp_ref[...] = direct.reshape(NZ, TR, PW)
    for d in ZD:
        send(dp_ref.at[zp(d)], rz_ref.at[d - 1], dz_sems.at[d - 1], to_z(d), OUT_D)

    for d in XD:
        send(mpa_ref.at[core, xp(d)], ax_ref.at[d - 1], ma_sems.at[d], to_x(d), OUT_MA)

    ksum = ks_ref[x]
    for d in XD:
        arrive(kx_ref.at[d - 1], k_sems.at[d])
        ksum = ksum + kx_ref[d - 1]
    ks_ref[x] = ksum
    for d in YD:
        @pl.when(yp(d) < NP)
        def _():
            pltpu.make_async_remote_copy(
                src_ref=ks_ref.at[x, lax.min(yp(d), NP - 1)], dst_ref=ky_ref.at[d - 1],
                send_sem=ky_out_sems.at[d], recv_sem=k_sems.at[NX + d],
                device_id=to_y(d), device_id_type=pl.DeviceIdType.MESH).start()

    part = mpb_ref[core, y]
    for d in YD:
        arrive(by_ref.at[d - 1], mb_sems.at[d])
        part = part + by_ref[d - 1]
    bs_ref[...] = part
    for d in XD:
        send(bs_ref.at[xp(d)], bx_ref.at[d - 1], mb_sems.at[NY + d], to_x(d), OUT_MB)

    part = mpa_ref[core, x]
    for d in XD:
        arrive(ax_ref.at[d - 1], ma_sems.at[d])
        part = part + ax_ref[d - 1]
    mpa_ref[core, x] = part
    for d in YD:
        send(mpa_ref.at[core, x, yp(d)], ay_ref.at[d - 1], ma_sems.at[NX + d], to_y(d), OUT_MA)

    own_g = g_ref.at[own_l, :, core]

    @pl.when(holds_g)
    def _():
        for d in ZD:
            arrive(g_ref.at[own_l, zp(NZ - d), core], gz_sems.at[d - 1])
        for d in XD:
            send(own_g, own_g, ga_sems.at[d], to_x(d), OUT_GX)

    held = y < NP
    yy = lax.min(y, NP - 1)

    @pl.when(held)
    def _():
        ksum = ks_ref[x, yy]
        for d in YD:
            arrive(ky_ref.at[d - 1], k_sems.at[NX + d])
            ksum = ksum + ky_ref[d - 1]
        kf_ref[...] = ksum
        for d in ZD:
            send(kf_ref, kz_ref.at[d - 1], kz_sems.at[d - 1], to_z(d), OUT_KZ)

    part_b = bs_ref[x]
    for d in XD:
        arrive(bx_ref.at[d - 1], mb_sems.at[NY + d])
        part_b = part_b + bx_ref[d - 1]
    part_a = mpa_ref[core, x, y]
    for d in YD:
        arrive(ay_ref.at[d - 1], ma_sems.at[NX + d])
        part_a = part_a + ay_ref[d - 1]
    wsum = dp_ref[z]
    for d in ZD:
        arrive(rz_ref.at[d - 1], dz_sems.at[d - 1])
        wsum = wsum + rz_ref[d - 1]
    wr_ref[z, :, :LA] = wsum[:, :LA] + part_a
    wr_ref[z, :, LA:] = wsum[:, LA:] + part_b
    wc_ref[x, y, core] = wr_ref[z]
    own_w = wc_ref.at[x, y, core]
    for d in YD:
        send(own_w, own_w, w_sems.at[d], to_y(d), OUT_W)
    for d in XD:
        send(own_w, own_w, w_sems.at[NY + d], to_x(d), OUT_W)
    for d in ZD:
        send(wr_ref.at[z], wr_ref.at[z], wz_sems.at[d - 1], to_z(d), OUT_W)

    for d in XD:
        src_l = xp(NX - d)

        @pl.when(src_l < NL)
        def _():
            arrive(g_ref.at[lax.min(src_l, NL - 1), :, core], ga_sems.at[d])
    send(g_ref.at[:, :, core], g_ref.at[:, :, core], ga_sems.at[0], to_core, OUT_GC)

    arrive(g_ref.at[:, :, other], ga_sems.at[0])
    whole = jnp.concatenate([g_ref[l].reshape(PW, LW) for l in range(NL)], axis=1)
    scaled, eye, s_row, s_col, start = scaled_gram(whole)
    sg_ref[...] = scaled
    inv_ref[...] = start

    def newton(dot):
        residual = eye - dot(sg_ref[...], inv_ref[...])
        inv_ref[...] += dot(inv_ref[...], residual)

    coarse = lambda a, b: jnp.dot(a.astype(jnp.bfloat16), b.astype(jnp.bfloat16),
                                  preferred_element_type=jnp.float32)
    fine = lambda a, b: dot_split(a, b, NN)

    for n, d in enumerate(YD):
        tile = wc_ref.at[x, yp(NY - d), core]
        arrive(tile, w_sems.at[d])
        for dx in XD:
            send(tile, tile, w_sems.at[NY + dx], to_x(dx), OUT_W)
        if n < COARSE_STEPS:
            newton(coarse)
    send(wc_ref.at[x, :, core], wc_ref.at[x, :, core], w_sems.at[NY + NX], to_core, OUT_W)
    for _ in range(COARSE_STEPS - len(YD)):
        newton(coarse)

    own_k = k_ref.at[core, x, yy]

    @pl.when(held)
    def _():
        ksum = kf_ref[...]
        for d in ZD:
            arrive(kz_ref.at[d - 1], kz_sems.at[d - 1])
            ksum = ksum + kz_ref[d - 1]
        k_ref[core, x, yy] = ksum
        for d in YD:
            send(own_k, own_k, ka_sems.at[d], to_y(d), OUT_KY)
    newton(fine)
    newton(fine)

    def pass_w(dx):
        block = wc_ref.at[xp(NX - dx), :, core]
        arrive(block, w_sems.at[NY + dx])
        send(block, block, w_sems.at[NY + NX + dx], to_core, OUT_W)

    pass_w(XD[0])

    for d in YD:
        src_y = yp(NY - d)

        @pl.when(src_y < NP)
        def _():
            arrive(k_ref.at[core, x, lax.min(src_y, NP - 1)], ka_sems.at[d])
    for d in XD:
        send(k_ref.at[core, x], k_ref.at[core, x], ka_sems.at[NY + d], to_x(d), OUT_K)
    for dx in XD[1:]:
        pass_w(dx)
    newton(fine)
    for d in XD:
        arrive(k_ref.at[core, xp(NX - d)], ka_sems.at[NY + d])
    send(k_ref.at[core], k_ref.at[core], ka_sems.at[0], to_core, OUT_K)

    residual = eye - dot_nn(sg_ref[...], inv_ref[...])
    err_ref[...] = jnp.full(err_ref.shape, jnp.sum(residual * residual), jnp.float32)
    inv_ref[...] = (inv_ref[...] + fine(inv_ref[...], residual)) * s_row * s_col

    for d in ZD:
        arrive(wr_ref.at[zp(NZ - d)], wz_sems.at[d - 1])
    arrive(wc_ref.at[x, :, other], w_sems.at[NY + NX])
    for dx in XD:
        arrive(wc_ref.at[xp(NX - dx), :, other], w_sems.at[NY + NX + dx])
    arrive(k_ref.at[other], ka_sems.at[0])
    for out in (OUT_T, OUT_W, OUT_MA, OUT_MB, OUT_D, OUT_K):
        all_left(out)
    left(g_ref.at[:, :, core], out_sems.at[OUT_GC])
    left(gc_ref, out_sems.at[OUT_G])
    for d in XD:
        pl.when(xp(d) < NL)(functools.partial(left, gx_ref.at[d - 1], ky_out_sems.at[NY + d]))
    for d in YD:
        pl.when(yp(d) < NP)(functools.partial(left, ky_ref.at[d - 1], ky_out_sems.at[d]))

    @pl.when(held)
    def _():
        all_left(OUT_KZ)
        all_left(OUT_KY)

    @pl.when(holds_g)
    def _():
        all_left(OUT_GS)
        all_left(OUT_GX)


def exchange(matrix, panel, sizes):
    NX, NY, NZ, TR, WIDTH, PW, NL, LA = sizes
    f32 = jnp.float32
    NP = PW // 2 // NX // 8
    GR = PW // NZ // 2
    LW, LB = PW // NL, PW - LA
    vmem = pl.BlockSpec(memory_space=pltpu.VMEM)
    shape = lambda *s: jax.ShapeDtypeStruct(s, f32)
    V = lambda *s: pltpu.VMEM(s, f32)
    D = lambda n: pltpu.SemaphoreType.DMA((n,))
    return pl.pallas_call(
        functools.partial(comm_kernel, sizes),
        out_shape=[shape(NL, NZ, 2, GR, LW), shape(2, NX, NP, 8, PW), shape(NX, NY, 2, TR, PW),
                   shape(NX, NY, 2, TR, PW), shape(NZ, TR, PW), shape(PW, PW), shape(8, 128)],
        in_specs=[pl.BlockSpec(memory_space=pltpu.HBM)] * 2,
        out_specs=[vmem] * 7,
        scratch_shapes=[
            V(NZ, TR, WIDTH), V(NZ, TR, PW), V(PW, PW), V(160, 8, PW), V(NZ, TR, WIDTH),
            V(NL, NZ, 2, GR, LW), V(NL, GR, LW), V(NL, GR, LW), V(NX - 1, GR, LW), V(GR, LW),
            V(NY - 1, GR, LW),
            V(2, NX, NY, TR, LA), V(2, NY, NX, TR, LB), V(NX, NY, TR, LA), V(NY, NX, TR, LB),
            V(NX - 1, NY, TR, LA), V(NY - 1, TR, LA), V(NY - 1, NX, TR, LB), V(NX, TR, LB),
            V(NX - 1, TR, LB),
            V(NZ, TR, PW), V(NZ - 1, TR, PW), V(2, NX, NP, 8, PW), V(NX, NP, 8, PW),
            V(NX - 1, NP, 8, PW), V(NX, NP, 8, PW), V(NY - 1, 8, PW), V(NZ - 1, 8, PW), V(8, PW),
            D(2), D(12), D(NY + NX), D(NY + 2 * NX), D(NY + 2 * NX), D(NZ - 1), D(NX + NY), D(NX + NY),
            D(NZ - 1), D(NX + NY), D(NZ - 1), D(NX), D(NX + NY), D(NZ - 1), D(NX + NY),
        ],
        compiler_params=pltpu.CompilerParams(
            collective_id=0, has_side_effects=True, vmem_limit_bytes=32 * 2**20),
        name="exchange",
    )(matrix, panel)


def polish(g_ref, n_ref, error):
    blocks, _, _, _, width = g_ref.shape
    size = blocks * width
    gram = jnp.concatenate([g_ref[l].reshape(size, width) for l in range(blocks)], axis=1)
    scaled, eye, s_row, s_col, start = scaled_gram(gram)
    usable = error < 0.25
    guess = n_ref[...] / s_row / s_col

    def step(state):
        count, _, guess = state
        residual = eye - dot_nn(scaled, guess)
        error = jnp.sum(residual * residual)
        return count + 1, error, guess + dot_nn(guess, residual)

    def again(state):
        return jnp.logical_and(state[1] > 1e-8, state[0] < 80)

    state = (0, jnp.where(usable, error, 1.0), jnp.where(usable, guess, start))
    _, _, found = lax.while_loop(again, step, state)
    n_ref[...] = found * s_row * s_col


def finish_kernel(mat_ref, pan_ref, g_ref, k_ref, tc_ref, wc_ref, wr_ref, inv_ref, err_ref, out_ref, n_ref):
    NZ, TR, WIDTH = mat_ref.shape
    PW = pan_ref.shape[2]
    row = lax.axis_index("row")
    z = lax.axis_index("col")
    n_ref[...] = inv_ref[...]
    error = err_ref[0, 0]

    @pl.when(jnp.logical_not(error <= 1e-8))
    def _():
        polish(g_ref, n_ref, error)

    inv = n_ref[...]
    half = k_ref[...]
    proj = half + half.T
    t_rows = pan_ref[...].reshape(NZ * TR, PW)
    w_rows = wr_ref[...].reshape(NZ * TR, PW)
    left = dot_nn(t_rows, inv)
    right = dot_nn(w_rows - 2.0 * dot_nn(left, proj), inv)
    sub = lax.broadcasted_iota(jnp.int32, (TR, WIDTH), 0) + row * TR
    lane = lax.broadcasted_iota(jnp.int32, (TR, WIDTH), 1)
    change = dot_split(left, wc_ref[...], NT) + dot_split(right, tc_ref[...], NT)
    change = change.reshape(NZ, TR, WIDTH)
    for a in range(NZ):
        new = mat_ref[a] - 2.0 * change[a]
        keep = jnp.logical_or(z < a, jnp.logical_and(z == a, sub >= lane))
        out_ref[a] = jnp.where(keep, new, 0.0)


def finish(*operands):
    matrix = operands[0]
    vmem = pl.BlockSpec(memory_space=pltpu.VMEM)
    return pl.pallas_call(
        finish_kernel,
        out_shape=jax.ShapeDtypeStruct(matrix.shape, jnp.float32),
        in_specs=[vmem] * len(operands),
        out_specs=vmem,
        scratch_shapes=[pltpu.VMEM(operands[7].shape, jnp.float32)],
        compiler_params=pltpu.CompilerParams(vmem_limit_bytes=32 * 2**20),
        name="finish",
    )(*operands)


def per_device(matrix, panel):
    NZ, _, TR, WIDTH = matrix.shape
    PW = panel.shape[3]
    NX, NY = PLANES[lax.axis_size("row")]
    lanes = max(PW // 128, 1)
    sizes = (NX, NY, NZ, TR, WIDTH, PW, lanes, PW // lanes if lanes > 1 else PW // 2)
    mat = matrix.reshape(NZ, TR, WIDTH)
    pan = panel.reshape(NZ, TR, PW)
    gram, proj, t_cols, w_cols, w_rows, guess, error = exchange(mat, pan, sizes)
    out = finish(mat, pan, gram, proj.reshape(PW, PW),
                 t_cols.reshape(WIDTH, PW), w_cols.reshape(WIDTH, PW), w_rows, guess, error)
    return out.reshape(NZ, 1, TR, WIDTH)


def solution(mesh):
    in_specs = (P(None, "row", None, "col"), P(None, "row", None, None))
    out_specs = P(None, "row", None, "col")
    return jax.shard_map(
        per_device, mesh=mesh, in_specs=in_specs, out_specs=out_specs, check_vma=False)
```

time: 91.3 us -> 76.4 us (0.84)
  Pallas kernels: 89 us -> 74.1 us
    pallas_call x1, Pallas kernels: 83.7 us -> 69.2 us  [exchange(): pl.pallas_call(functools.partial(comm_kernel, sizes), out_shape=[shape(NL...]
where the time goes in v3:
time: 76.4 us; the launch traced here: 76.2 us
  Pallas kernels  74.1 us (97%)
  local copies, waits for them, and re-layouts  2.09 us (3%)
    pallas_call x1, Pallas kernels, exchange(): pl.pallas_call(functools.partial(comm_kernel, sizes), out_shape=[shape(NL...  69.2 us
    pallas_call x1, Pallas kernels, finish(): pl.pallas_call(finish_kernel, out_shape=jax.ShapeDtypeStruct(matrix.shape...  4.88 us
    unnamed x4, local copies, waits for them, and re-layouts  2.09 us

profile of v3, /device:TPU:1, one launch (start us, length us, event | category | flops | bytes accessed | tf_op | source)
XLA Modules:
  0.0 76.2 jit_solution(15328901361556034488)
XLA Ops:
  0.0 0.0 copy-start
  0.0 1.1 %copy-done = f32[12,1,16,1024]{3,2,1,0:T(8,128)S(1)} copy-done((f32[12,1,16,1024]{3,2,1,0:T(8,128)S(1)}, f32[12,1,16,1024]{3,2,1,0:T(8,128)}, u32[]{:S(2)}) %copy-start) | copy-done | bytes 786456
  1.1 0.0 copy-start.1
  1.1 1.0 %copy-done.1 = f32[12,1,16,384]{3,2,1,0:T(8,128)S(1)} copy-done((f32[12,1,16,384]{3,2,1,0:T(8,128)S(1)}, f32[12,1,16,384]{3,2,1,0:T(8,128)}, u32[]{:S(2)}) %copy-start.1) | copy-done | bytes 294936
  2.1 69.2 %exchange.1 = (f32[3,12,2,16,128]{4,3,2,1,0:T(8,128)S(1)}, f32[2,4,6,8,384]{4,3,2,1,0:T(8,128)S(1)}, f32[4,8,2,16,384]{4,3,2,1,0:T(8,128)S(1)}, f32[4,8,2,16,384...) custom-call(f32[12,16,1024]{2,1,0:T(8,128)S(1)} %bitcast.8, ...), custom_call_target="tpu_custom_call" | custom-call | tf_op jit(solution)/shard_map/exchange/pallas_call | solution.py:442
  71.3 4.9 %finish.1 = f32[12,16,1024]{2,1,0:T(8,128)} custom-call(f32[12,16,1024]{2,1,0:T(8,128)S(1)} %bitcast.9, f32[12,16,384]{2,1,0:T(8,128)S(1)} %bitcast.13, f32[3,12,2,16,128]{4,3,2,1,0:T(8,128)S(1)} %get-tuple-element.12.g_ref, f32[384,384]{1,0:T(8,128)S(1)} %bitcast.14, f32[1024,384]{1,0:T(8,128)S(1)} %bitcast.10, f32[1024,384]{1,0:T(8,128)S(1)} %bitcast.11, ...), custom_call_target="tpu_custom_call" | custom-call | tf_op jit(solution)/shard_map/finish/pallas_call | solution.py:520
Async XLA Ops:
  0.0 1.1 %copy-start = (f32[12,1,16,1024]{3,2,1,0:T(8,128)S(1)}, f32[12,1,16,1024]{3,2,1,0:T(8,128)}, u32[]{:S(2)}) copy-start(f32[12,1,16,1024]{3,2,1,0:T(8,128)} %param.2) | copy-start | bytes 2359300
  1.1 1.0 %copy-start.1 = (f32[12,1,16,384]{3,2,1,0:T(8,128)S(1)}, f32[12,1,16,384]{3,2,1,0:T(8,128)}, u32[]{:S(2)}) copy-start(f32[12,1,16,384]{3,2,1,0:T(8,128)} %param.3) | copy-start | bytes 884740

commit v4 on v3

--- a/solution.py
+++ b/solution.py
@@ -58,9 +58,10 @@
 
 
 COARSE_STEPS = 4
-
-
-def comm_kernel(sizes, mat_hbm, pan_hbm, g_ref, k_ref, tc_ref, wc_ref, wr_ref, inv_ref, err_ref,
+KR = 16
+
+
+def comm_kernel(sizes, mat_hbm, pan_hbm, g_ref, k_ref, tc_ref, wc_ref, wr_ref, inv_ref, err_ref, left_ref,
                 mat_ref, pan_ref, sg_ref, units_ref, h_ref,
                 gl_ref, gc_ref, gsum_ref, gx_ref, gsx_ref, gy_ref,
                 mpa_ref, mpb_ref, ca_ref, cb_ref, ax_ref, ay_ref, by_ref, bs_ref, bx_ref,
@@ -68,8 +69,9 @@
                 in_sems, out_sems, ky_out_sems, t_sems, w_sems, wz_sems, ma_sems, mb_sems, dz_sems,
                 g_sems, gz_sems, ga_sems, k_sems, kz_sems, ka_sems):
     NX, NY, NZ, TR, WIDTH, PW, NL, LA = sizes
-    NP = PW // 2 // NX // 8
     LW = PW // NL
+    PAIRS = [(i, j) for i in range(NL) for j in range(i + 1)]
+    NP = len(PAIRS) * LW // 2 // NX // KR
     row = lax.axis_index("row")
     z = lax.axis_index("col")
     core = lax.rem(row, 2)
@@ -131,7 +133,7 @@
             src_ref=dst, dst_ref=dst, send_sem=out_sems.at[0], recv_sem=sem,
             device_id=to_core, device_id_type=pl.DeviceIdType.MESH).wait_recv()
 
-    OUT_T, OUT_W, OUT_MA, OUT_MB, OUT_D, OUT_K, OUT_KZ, OUT_KY, OUT_G, OUT_GS, OUT_GX, OUT_GC = range(12)
+    OUT_T, OUT_W, OUT_MA, OUT_MB, OUT_D, OUT_K, OUT_KZ, OUT_KY, OUT_G, OUT_GS, OUT_GX, OUT_GC, OUT_KX = range(13)
     YD, XD, ZD = by_distance(NY), by_distance(NX), by_distance(NZ)
 
     pan_in.wait()
@@ -233,8 +235,10 @@
                 own_g = g_ref.at[own_l, z, core]
                 for d in ZD:
                     send(own_g, own_g, gz_sems.at[d - 1], to_z(d), OUT_GS)
-    kp_ref[:, :, :, :, :LA] = ka.reshape(2, NX, NP, 8, LA)
-    kp_ref[:, :, :, :, LA:] = kb.reshape(2, NX, NP, 8, PW - LA)
+    terms = jnp.concatenate([ka, kb], axis=1)
+    block = lambda i, j: terms[i * LW:(i + 1) * LW, j * LW:(j + 1) * LW]
+    lower = [block(i, j) + block(j, i).T for i, j in PAIRS]
+    kp_ref[...] = jnp.concatenate(lower, axis=0).reshape(2, NX, NP, KR, LW)
     send(kp_ref.at[other], kc_ref, k_sems.at[0], to_core, OUT_K)
 
     arrive(tc_ref.at[x, :, other], t_sems.at[NY + NX])
@@ -374,44 +378,58 @@
         k_ref[core, x, yy] = ksum
         for d in YD:
             send(own_k, own_k, ka_sems.at[d], to_y(d), OUT_KY)
-    newton(fine)
-    newton(fine)
+        for d in XD:
+            send(own_k, own_k, ka_sems.at[NY + d], to_x(d), OUT_KX)
+
+    def forward_k(ds):
+        for d in ds:
+            src_y = yp(NY - d)
+
+            @pl.when(src_y < NP)
+            def _():
+                piece = k_ref.at[core, x, lax.min(src_y, NP - 1)]
+                arrive(piece, ka_sems.at[d])
+                for dx in XD:
+                    send(piece, piece, ka_sems.at[NY + dx], to_x(dx), OUT_KX)
 
     def pass_w(dx):
         block = wc_ref.at[xp(NX - dx), :, core]
         arrive(block, w_sems.at[NY + dx])
         send(block, block, w_sems.at[NY + NX + dx], to_core, OUT_W)
 
-    pass_w(XD[0])
-
-    for d in YD:
-        src_y = yp(NY - d)
-
-        @pl.when(src_y < NP)
-        def _():
-            arrive(k_ref.at[core, x, lax.min(src_y, NP - 1)], ka_sems.at[d])
-    for d in XD:
-        send(k_ref.at[core, x], k_ref.at[core, x], ka_sems.at[NY + d], to_x(d), OUT_K)
-    for dx in XD[1:]:
+    def pass_k(dx):
+        block = k_ref.at[core, xp(NX - dx)]
+        if dx:
+            arrive(block, ka_sems.at[NY + dx])
+        send(block, block, ka_sems.at[NY + NX + dx], to_core, OUT_K)
+
+    newton(fine)
+    forward_k(YD[:3])
+    newton(fine)
+    forward_k(YD[3:])
+    pass_k(0)
+    for dx in XD:
         pass_w(dx)
     newton(fine)
-    for d in XD:
-        arrive(k_ref.at[core, xp(NX - d)], ka_sems.at[NY + d])
-    send(k_ref.at[core], k_ref.at[core], ka_sems.at[0], to_core, OUT_K)
+    for dx in XD:
+        pass_k(dx)
 
     residual = eye - dot_nn(sg_ref[...], inv_ref[...])
     err_ref[...] = jnp.full(err_ref.shape, jnp.sum(residual * residual), jnp.float32)
     inv_ref[...] = (inv_ref[...] + fine(inv_ref[...], residual)) * s_row * s_col
+    left_ref[...] = dot_nn(pan_ref[...].reshape(NZ * TR, PW), inv_ref[...])
 
     for d in ZD:
         arrive(wr_ref.at[zp(NZ - d)], wz_sems.at[d - 1])
     arrive(wc_ref.at[x, :, other], w_sems.at[NY + NX])
     for dx in XD:
         arrive(wc_ref.at[xp(NX - dx), :, other], w_sems.at[NY + NX + dx])
-    arrive(k_ref.at[other], ka_sems.at[0])
+    for dx in [0] + XD:
+        arrive(k_ref.at[other, xp(NX - dx)], ka_sems.at[NY + NX + dx])
     for out in (OUT_T, OUT_W, OUT_MA, OUT_MB, OUT_D, OUT_K):
         all_left(out)
     left(g_ref.at[:, :, core], out_sems.at[OUT_GC])
+    left(kx_ref, out_sems.at[OUT_KX])
     left(gc_ref, out_sems.at[OUT_G])
     for d in XD:
         pl.when(xp(d) < NL)(functools.partial(left, gx_ref.at[d - 1], ky_out_sems.at[NY + d]))
@@ -420,8 +438,8 @@
 
     @pl.when(held)
     def _():
-        all_left(OUT_KZ)
-        all_left(OUT_KY)
+        left(kz_ref, out_sems.at[OUT_KZ])
+        left(ky_ref, out_sems.at[OUT_KY])
 
     @pl.when(holds_g)
     def _():
@@ -432,19 +450,20 @@
 def exchange(matrix, panel, sizes):
     NX, NY, NZ, TR, WIDTH, PW, NL, LA = sizes
     f32 = jnp.float32
-    NP = PW // 2 // NX // 8
     GR = PW // NZ // 2
     LW, LB = PW // NL, PW - LA
+    NP = NL * (NL + 1) // 2 * LW // 2 // NX // KR
     vmem = pl.BlockSpec(memory_space=pltpu.VMEM)
     shape = lambda *s: jax.ShapeDtypeStruct(s, f32)
     V = lambda *s: pltpu.VMEM(s, f32)
     D = lambda n: pltpu.SemaphoreType.DMA((n,))
     return pl.pallas_call(
         functools.partial(comm_kernel, sizes),
-        out_shape=[shape(NL, NZ, 2, GR, LW), shape(2, NX, NP, 8, PW), shape(NX, NY, 2, TR, PW),
-                   shape(NX, NY, 2, TR, PW), shape(NZ, TR, PW), shape(PW, PW), shape(8, 128)],
+        out_shape=[shape(NL, NZ, 2, GR, LW), shape(2, NX, NP, KR, LW), shape(NX, NY, 2, TR, PW),
+                   shape(NX, NY, 2, TR, PW), shape(NZ, TR, PW), shape(PW, PW), shape(8, 128),
+                   shape(NZ * TR, PW)],
         in_specs=[pl.BlockSpec(memory_space=pltpu.HBM)] * 2,
-        out_specs=[vmem] * 7,
+        out_specs=[vmem] * 8,
         scratch_shapes=[
             V(NZ, TR, WIDTH), V(NZ, TR, PW), V(PW, PW), V(160, 8, PW), V(NZ, TR, WIDTH),
             V(NL, NZ, 2, GR, LW), V(NL, GR, LW), V(NL, GR, LW), V(NX - 1, GR, LW), V(GR, LW),
@@ -452,10 +471,10 @@
             V(2, NX, NY, TR, LA), V(2, NY, NX, TR, LB), V(NX, NY, TR, LA), V(NY, NX, TR, LB),
             V(NX - 1, NY, TR, LA), V(NY - 1, TR, LA), V(NY - 1, NX, TR, LB), V(NX, TR, LB),
             V(NX - 1, TR, LB),
-            V(NZ, TR, PW), V(NZ - 1, TR, PW), V(2, NX, NP, 8, PW), V(NX, NP, 8, PW),
-            V(NX - 1, NP, 8, PW), V(NX, NP, 8, PW), V(NY - 1, 8, PW), V(NZ - 1, 8, PW), V(8, PW),
-            D(2), D(12), D(NY + NX), D(NY + 2 * NX), D(NY + 2 * NX), D(NZ - 1), D(NX + NY), D(NX + NY),
-            D(NZ - 1), D(NX + NY), D(NZ - 1), D(NX), D(NX + NY), D(NZ - 1), D(NX + NY),
+            V(NZ, TR, PW), V(NZ - 1, TR, PW), V(2, NX, NP, KR, LW), V(NX, NP, KR, LW),
+            V(NX - 1, NP, KR, LW), V(NX, NP, KR, LW), V(NY - 1, KR, LW), V(NZ - 1, KR, LW), V(KR, LW),
+            D(2), D(13), D(NY + NX), D(NY + 2 * NX), D(NY + 2 * NX), D(NZ - 1), D(NX + NY), D(NX + NY),
+            D(NZ - 1), D(NX + NY), D(NZ - 1), D(NX), D(NX + NY), D(NZ - 1), D(2 * NX + NY),
         ],
         compiler_params=pltpu.CompilerParams(
             collective_id=0, has_side_effects=True, vmem_limit_bytes=32 * 2**20),
@@ -485,25 +504,32 @@
     n_ref[...] = found * s_row * s_col
 
 
-def finish_kernel(mat_ref, pan_ref, g_ref, k_ref, tc_ref, wc_ref, wr_ref, inv_ref, err_ref, out_ref, n_ref):
+def finish_kernel(mat_ref, pan_ref, g_ref, k_ref, tc_ref, wc_ref, wr_ref, inv_ref, err_ref, left_ref,
+                  out_ref, n_ref, tn_ref):
     NZ, TR, WIDTH = mat_ref.shape
     PW = pan_ref.shape[2]
     row = lax.axis_index("row")
     z = lax.axis_index("col")
     n_ref[...] = inv_ref[...]
+    tn_ref[...] = left_ref[...]
     error = err_ref[0, 0]
+    t_rows = pan_ref[...].reshape(NZ * TR, PW)
 
     @pl.when(jnp.logical_not(error <= 1e-8))
     def _():
         polish(g_ref, n_ref, error)
-
-    inv = n_ref[...]
-    half = k_ref[...]
-    proj = half + half.T
-    t_rows = pan_ref[...].reshape(NZ * TR, PW)
+        tn_ref[...] = dot_nn(t_rows, n_ref[...])
+
+    size = k_ref.shape[-1]
+    count = PW // size
+    lower = k_ref[...].reshape(-1, size)
+    block = lambda i, j: lower[(i * (i + 1) // 2 + j) * size:(i * (i + 1) // 2 + j + 1) * size]
+    proj = jnp.concatenate([
+        jnp.concatenate([block(i, j) if i >= j else block(j, i).T for j in range(count)], axis=1)
+        for i in range(count)], axis=0)
+    left = tn_ref[...]
     w_rows = wr_ref[...].reshape(NZ * TR, PW)
-    left = dot_nn(t_rows, inv)
-    right = dot_nn(w_rows - 2.0 * dot_nn(left, proj), inv)
+    right = dot_split(w_rows - 2.0 * dot_split(left, proj, NN), n_ref[...], NN)
     sub = lax.broadcasted_iota(jnp.int32, (TR, WIDTH), 0) + row * TR
     lane = lax.broadcasted_iota(jnp.int32, (TR, WIDTH), 1)
     change = dot_split(left, wc_ref[...], NT) + dot_split(right, tc_ref[...], NT)
@@ -522,7 +548,7 @@
         out_shape=jax.ShapeDtypeStruct(matrix.shape, jnp.float32),
         in_specs=[vmem] * len(operands),
         out_specs=vmem,
-        scratch_shapes=[pltpu.VMEM(operands[7].shape, jnp.float32)],
+        scratch_shapes=[pltpu.VMEM(operands[7].shape, jnp.float32), pltpu.VMEM(operands[9].shape, jnp.float32)],
         compiler_params=pltpu.CompilerParams(vmem_limit_bytes=32 * 2**20),
         name="finish",
     )(*operands)
@@ -536,9 +562,9 @@
     sizes = (NX, NY, NZ, TR, WIDTH, PW, lanes, PW // lanes if lanes > 1 else PW // 2)
     mat = matrix.reshape(NZ, TR, WIDTH)
     pan = panel.reshape(NZ, TR, PW)
-    gram, proj, t_cols, w_cols, w_rows, guess, error = exchange(mat, pan, sizes)
-    out = finish(mat, pan, gram, proj.reshape(PW, PW),
-                 t_cols.reshape(WIDTH, PW), w_cols.reshape(WIDTH, PW), w_rows, guess, error)
+    gram, proj, t_cols, w_cols, w_rows, guess, error, left = exchange(mat, pan, sizes)
+    out = finish(mat, pan, gram, proj,
+                 t_cols.reshape(WIDTH, PW), w_cols.reshape(WIDTH, PW), w_rows, guess, error, left)
     return out.reshape(NZ, 1, TR, WIDTH)
 
 

time: 76.4 us -> 73.7 us (0.965)
  Pallas kernels: 74.1 us -> 71 us
    pallas_call x1, Pallas kernels: 69.2 us -> 67.5 us  [exchange(): pl.pallas_call(functools.partial(comm_kernel, sizes), out_shape=[shape(NL...]
    pallas_call x1, Pallas kernels: 4.88 us -> 3.41 us  [finish(): pl.pallas_call(finish_kernel, out_shape=jax.ShapeDtypeStruct(matrix.shape...]
where the time goes in v4:
time: 73.7 us; the launch traced here: 73.1 us
  Pallas kernels  71 us (96%)
  local copies, waits for them, and re-layouts  2.09 us (3%)
    pallas_call x1, Pallas kernels, exchange(): pl.pallas_call(functools.partial(comm_kernel, sizes), out_shape=[shape(NL...  67.5 us
    pallas_call x1, Pallas kernels, finish(): pl.pallas_call(finish_kernel, out_shape=jax.ShapeDtypeStruct(matrix.shape...  3.41 us
    unnamed x4, local copies, waits for them, and re-layouts  2.09 us

profile of v4, /device:TPU:1, one launch (start us, length us, event | category | flops | bytes accessed | tf_op | source)
XLA Modules:
  0.0 73.1 jit_solution(17550205852623667266)
XLA Ops:
  0.0 0.0 copy-start
  0.0 1.1 %copy-done = f32[12,1,16,1024]{3,2,1,0:T(8,128)S(1)} copy-done((f32[12,1,16,1024]{3,2,1,0:T(8,128)S(1)}, f32[12,1,16,1024]{3,2,1,0:T(8,128)}, u32[]{:S(2)}) %copy-start) | copy-done | bytes 786456
  1.1 0.0 copy-start.1
  1.1 1.0 %copy-done.1 = f32[12,1,16,384]{3,2,1,0:T(8,128)S(1)} copy-done((f32[12,1,16,384]{3,2,1,0:T(8,128)S(1)}, f32[12,1,16,384]{3,2,1,0:T(8,128)}, u32[]{:S(2)}) %copy-start.1) | copy-done | bytes 294936
  2.1 67.5 %exchange.1 = (f32[3,12,2,16,128]{4,3,2,1,0:T(8,128)S(1)}, f32[2,4,6,16,128]{4,3,2,1,0:T(8,128)S(1)}, f32[4,8,2,16,384]{4,3,2,1,0:T(8,128)S(1)}, f32[4,8,2,16,38...) custom-call(f32[12,16,1024]{2,1,0:T(8,128)S(1)} %bitcast.7, ...), custom_call_target="tpu_custom_call" | custom-call | tf_op jit(solution)/shard_map/exchange/pallas_call | solution.py:460
  69.7 3.4 %finish.1 = f32[12,16,1024]{2,1,0:T(8,128)} custom-call(f32[12,16,1024]{2,1,0:T(8,128)S(1)} %bitcast.8, f32[12,16,384]{2,1,0:T(8,128)S(1)} %bitcast.12, f32[3,12,2,16,128]{4,3,2,1,0:T(8,128)S(1)} %get-tuple-element.13.g_ref, f32[2,4,6,16,128]{4,3,2,1,0:T(8,128)S(1)} %get-tuple-element.14.k_ref, f32[1024,384]{1,0:T(8,128)S(1)} %bitcast.9, ...), custom_call_target="tpu_custom_call" | custom-call | tf_op jit(solution)/shard_map/finish/pallas_call | solution.py:546
Async XLA Ops:
  0.0 1.1 %copy-start = (f32[12,1,16,1024]{3,2,1,0:T(8,128)S(1)}, f32[12,1,16,1024]{3,2,1,0:T(8,128)}, u32[]{:S(2)}) copy-start(f32[12,1,16,1024]{3,2,1,0:T(8,128)} %param.2) | copy-start | bytes 2359300
  1.1 1.0 %copy-start.1 = (f32[12,1,16,384]{3,2,1,0:T(8,128)S(1)}, f32[12,1,16,384]{3,2,1,0:T(8,128)}, u32[]{:S(2)}) copy-start(f32[12,1,16,384]{3,2,1,0:T(8,128)} %param.3) | copy-start | bytes 884740

commit v5 on v4

--- a/solution.py
+++ b/solution.py
@@ -57,16 +57,17 @@
     return scaled, eye, s_row, s_col, eye * (2.0 / (1.0 + bound))
 
 
-COARSE_STEPS = 4
+COARSE_STEPS = 5
+SMALL = 1e-6
 KR = 16
 
 
-def comm_kernel(sizes, mat_hbm, pan_hbm, g_ref, k_ref, tc_ref, wc_ref, wr_ref, inv_ref, err_ref, left_ref,
-                mat_ref, pan_ref, sg_ref, units_ref, h_ref,
+def comm_kernel(sizes, mat_ref, pan_ref, g_ref, k_ref, tc_ref, wc_ref, wr_ref, inv_ref, err_ref, left_ref,
+                sg_ref, units_ref, h_ref,
                 gl_ref, gc_ref, gsum_ref, gx_ref, gsx_ref, gy_ref,
                 mpa_ref, mpb_ref, ca_ref, cb_ref, ax_ref, ay_ref, by_ref, bs_ref, bx_ref,
                 dp_ref, rz_ref, kp_ref, kc_ref, kx_ref, ks_ref, ky_ref, kz_ref, kf_ref,
-                in_sems, out_sems, ky_out_sems, t_sems, w_sems, wz_sems, ma_sems, mb_sems, dz_sems,
+                out_sems, ky_out_sems, t_sems, w_sems, wz_sems, ma_sems, mb_sems, dz_sems,
                 g_sems, gz_sems, ga_sems, k_sems, kz_sems, ka_sems):
     NX, NY, NZ, TR, WIDTH, PW, NL, LA = sizes
     LW = PW // NL
@@ -103,11 +104,6 @@
     for peer in peers:
         pl.semaphore_signal(barrier, inc=1, device_id=peer, device_id_type=pl.DeviceIdType.MESH)
 
-    pan_in = pltpu.make_async_copy(pan_hbm, pan_ref, in_sems.at[0])
-    mat_in = pltpu.make_async_copy(mat_hbm, mat_ref, in_sems.at[1])
-    pan_in.start()
-    mat_in.start()
-
     totals = {}
 
     def send(src, dst, sem, peer, out):
@@ -136,19 +132,26 @@
     OUT_T, OUT_W, OUT_MA, OUT_MB, OUT_D, OUT_K, OUT_KZ, OUT_KY, OUT_G, OUT_GS, OUT_GX, OUT_GC, OUT_KX = range(13)
     YD, XD, ZD = by_distance(NY), by_distance(NX), by_distance(NZ)
 
-    pan_in.wait()
-    tc_ref[x, y, core] = pan_ref[z]
-    t_rows = pan_ref[...].reshape(NZ * TR, PW)
-    gram = dot_tn(t_rows, t_rows)
-    for l in range(NL):
-        gl_ref[l] = gram[:, l * LW:(l + 1) * LW].reshape(NZ, 2, PW // NZ // 2, LW)
-    mat_in.wait()
     sub = lax.broadcasted_iota(jnp.int32, (TR, WIDTH), 0) + row * TR
     lane = lax.broadcasted_iota(jnp.int32, (TR, WIDTH), 1)
     for a in range(NZ):
         tile = mat_ref[a]
         diag_part = jnp.where(sub > lane, tile, jnp.where(sub == lane, 0.5 * tile, 0.0))
         h_ref[a] = jnp.where(z < a, tile, jnp.where(z == a, diag_part, 0.0))
+    pl.semaphore_wait(barrier, len(peers))
+
+    own_t = pan_ref.at[z]
+    for d in YD:
+        send(own_t, tc_ref.at[x, y, core], t_sems.at[d], to_y(d), OUT_T)
+    for d in XD:
+        send(own_t, tc_ref.at[x, y, core], t_sems.at[NY + d], to_x(d), OUT_T)
+    tc_ref[x, y, core] = pan_ref[z]
+
+    t_rows = pan_ref[...].reshape(NZ * TR, PW)
+    gram = dot_tn(t_rows, t_rows)
+    for l in range(NL):
+        gl_ref[l] = gram[:, l * LW:(l + 1) * LW].reshape(NZ, 2, PW // NZ // 2, LW)
+    send(gl_ref.at[:, z, other], gc_ref, g_sems.at[0], to_core, OUT_G)
     XW = WIDTH // NX
 
     def columns(xb):
@@ -156,18 +159,10 @@
 
     for d in [0] + XD:
         xb = xp(d)
-        terms = dot_tn(columns(xb), t_rows).reshape(NY, 2, TR, PW)
+        terms = dot_split(columns(xb), t_rows, TN).reshape(NY, 2, TR, PW)
         for c in range(2):
             mpa_ref[c, xb] = terms[:, c, :, :LA]
             mpb_ref[c, :, xb] = terms[:, c, :, LA:]
-    pl.semaphore_wait(barrier, len(peers))
-
-    own_t = pan_ref.at[z]
-    for d in YD:
-        send(own_t, tc_ref.at[x, y, core], t_sems.at[d], to_y(d), OUT_T)
-    for d in XD:
-        send(own_t, tc_ref.at[x, y, core], t_sems.at[NY + d], to_x(d), OUT_T)
-    send(gl_ref.at[:, z, other], gc_ref, g_sems.at[0], to_core, OUT_G)
     send(mpb_ref.at[other], cb_ref, mb_sems.at[0], to_core, OUT_MB)
     send(mpa_ref.at[other], ca_ref, ma_sems.at[0], to_core, OUT_MA)
 
@@ -342,6 +337,20 @@
             arrive(g_ref.at[lax.min(src_l, NL - 1), :, core], ga_sems.at[d])
     send(g_ref.at[:, :, core], g_ref.at[:, :, core], ga_sems.at[0], to_core, OUT_GC)
 
+    own_k = k_ref.at[core, x, yy]
+
+    @pl.when(held)
+    def _():
+        ksum = kf_ref[...]
+        for d in ZD:
+            arrive(kz_ref.at[d - 1], kz_sems.at[d - 1])
+            ksum = ksum + kz_ref[d - 1]
+        k_ref[core, x, yy] = ksum
+        for d in YD:
+            send(own_k, own_k, ka_sems.at[d], to_y(d), OUT_KY)
+        for d in XD:
+            send(own_k, own_k, ka_sems.at[NY + d], to_x(d), OUT_KX)
+
     arrive(g_ref.at[:, :, other], ga_sems.at[0])
     whole = jnp.concatenate([g_ref[l].reshape(PW, LW) for l in range(NL)], axis=1)
     scaled, eye, s_row, s_col, start = scaled_gram(whole)
@@ -367,20 +376,6 @@
     for _ in range(COARSE_STEPS - len(YD)):
         newton(coarse)
 
-    own_k = k_ref.at[core, x, yy]
-
-    @pl.when(held)
-    def _():
-        ksum = kf_ref[...]
-        for d in ZD:
-            arrive(kz_ref.at[d - 1], kz_sems.at[d - 1])
-            ksum = ksum + kz_ref[d - 1]
-        k_ref[core, x, yy] = ksum
-        for d in YD:
-            send(own_k, own_k, ka_sems.at[d], to_y(d), OUT_KY)
-        for d in XD:
-            send(own_k, own_k, ka_sems.at[NY + d], to_x(d), OUT_KX)
-
     def forward_k(ds):
         for d in ds:
             src_y = yp(NY - d)
@@ -403,20 +398,17 @@
             arrive(block, ka_sems.at[NY + dx])
         send(block, block, ka_sems.at[NY + NX + dx], to_core, OUT_K)
 
-    newton(fine)
     forward_k(YD[:3])
     newton(fine)
     forward_k(YD[3:])
     pass_k(0)
-    for dx in XD:
-        pass_w(dx)
-    newton(fine)
-    for dx in XD:
-        pass_k(dx)
-
     residual = eye - dot_nn(sg_ref[...], inv_ref[...])
     err_ref[...] = jnp.full(err_ref.shape, jnp.sum(residual * residual), jnp.float32)
     inv_ref[...] = (inv_ref[...] + fine(inv_ref[...], residual)) * s_row * s_col
+    for dx in XD:
+        pass_w(dx)
+    for dx in XD:
+        pass_k(dx)
     left_ref[...] = dot_nn(pan_ref[...].reshape(NZ * TR, PW), inv_ref[...])
 
     for d in ZD:
@@ -462,10 +454,10 @@
         out_shape=[shape(NL, NZ, 2, GR, LW), shape(2, NX, NP, KR, LW), shape(NX, NY, 2, TR, PW),
                    shape(NX, NY, 2, TR, PW), shape(NZ, TR, PW), shape(PW, PW), shape(8, 128),
                    shape(NZ * TR, PW)],
-        in_specs=[pl.BlockSpec(memory_space=pltpu.HBM)] * 2,
+        in_specs=[vmem] * 2,
         out_specs=[vmem] * 8,
         scratch_shapes=[
-            V(NZ, TR, WIDTH), V(NZ, TR, PW), V(PW, PW), V(160, 8, PW), V(NZ, TR, WIDTH),
+            V(PW, PW), V(160, 8, PW), V(NZ, TR, WIDTH),
             V(NL, NZ, 2, GR, LW), V(NL, GR, LW), V(NL, GR, LW), V(NX - 1, GR, LW), V(GR, LW),
             V(NY - 1, GR, LW),
             V(2, NX, NY, TR, LA), V(2, NY, NX, TR, LB), V(NX, NY, TR, LA), V(NY, NX, TR, LB),
@@ -473,7 +465,7 @@
             V(NX - 1, TR, LB),
             V(NZ, TR, PW), V(NZ - 1, TR, PW), V(2, NX, NP, KR, LW), V(NX, NP, KR, LW),
             V(NX - 1, NP, KR, LW), V(NX, NP, KR, LW), V(NY - 1, KR, LW), V(NZ - 1, KR, LW), V(KR, LW),
-            D(2), D(13), D(NY + NX), D(NY + 2 * NX), D(NY + 2 * NX), D(NZ - 1), D(NX + NY), D(NX + NY),
+            D(13), D(NY + NX), D(NY + 2 * NX), D(NY + 2 * NX), D(NZ - 1), D(NX + NY), D(NX + NY),
             D(NZ - 1), D(NX + NY), D(NZ - 1), D(NX), D(NX + NY), D(NZ - 1), D(2 * NX + NY),
         ],
         compiler_params=pltpu.CompilerParams(
@@ -497,7 +489,7 @@
         return count + 1, error, guess + dot_nn(guess, residual)
 
     def again(state):
-        return jnp.logical_and(state[1] > 1e-8, state[0] < 80)
+        return jnp.logical_and(state[1] > SMALL, state[0] < 80)
 
     state = (0, jnp.where(usable, error, 1.0), jnp.where(usable, guess, start))
     _, _, found = lax.while_loop(again, step, state)
@@ -515,7 +507,7 @@
     error = err_ref[0, 0]
     t_rows = pan_ref[...].reshape(NZ * TR, PW)
 
-    @pl.when(jnp.logical_not(error <= 1e-8))
+    @pl.when(jnp.logical_not(error <= SMALL))
     def _():
         polish(g_ref, n_ref, error)
         tn_ref[...] = dot_nn(t_rows, n_ref[...])

time: 73.7 us -> 74.5 us (1.011)
  Pallas kernels: 71 us -> 72.2 us
    pallas_call x1, Pallas kernels: 67.5 us -> 68.8 us  [exchange(): pl.pallas_call(functools.partial(comm_kernel, sizes), out_shape=[shape(NL...]
where the time goes in v5:
time: 74.5 us; the launch traced here: 74.3 us
  Pallas kernels  72.2 us (97%)
  local copies, waits for them, and re-layouts  2.09 us (3%)
    pallas_call x1, Pallas kernels, exchange(): pl.pallas_call(functools.partial(comm_kernel, sizes), out_shape=[shape(NL...  68.8 us
    pallas_call x1, Pallas kernels, finish(): pl.pallas_call(finish_kernel, out_shape=jax.ShapeDtypeStruct(matrix.shape...  3.4 us
    unnamed x4, local copies, waits for them, and re-layouts  2.09 us

profile of v5, /device:TPU:1, one launch (start us, length us, event | category | flops | bytes accessed | tf_op | source)
XLA Modules:
  0.0 74.3 jit_solution(3417599649005968917)
XLA Ops:
  0.0 0.0 copy-start
  0.0 1.1 %copy-done = f32[12,1,16,1024]{3,2,1,0:T(8,128)S(1)} copy-done((f32[12,1,16,1024]{3,2,1,0:T(8,128)S(1)}, f32[12,1,16,1024]{3,2,1,0:T(8,128)}, u32[]{:S(2)}) %copy-start) | copy-done | bytes 786456
  1.1 0.0 copy-start.1
  1.1 1.0 %copy-done.1 = f32[12,1,16,384]{3,2,1,0:T(8,128)S(1)} copy-done((f32[12,1,16,384]{3,2,1,0:T(8,128)S(1)}, f32[12,1,16,384]{3,2,1,0:T(8,128)}, u32[]{:S(2)}) %copy-start.1) | copy-done | bytes 294936
  2.1 68.8 %exchange.1 = (f32[3,12,2,16,128]{4,3,2,1,0:T(8,128)S(1)}, f32[2,4,6,16,128]{4,3,2,1,0:T(8,128)S(1)}, f32[4,8,2,16,384]{4,3,2,1,0:T(8,128)S(1)}, f32[4,8,2,16,38...) custom-call(f32[12,16,1024]{2,1,0:T(8,128)S(1)} %bitcast.7, ...), custom_call_target="tpu_custom_call" | custom-call | tf_op jit(solution)/shard_map/exchange/pallas_call | solution.py:452
  70.9 3.4 %finish.1 = f32[12,16,1024]{2,1,0:T(8,128)} custom-call(f32[12,16,1024]{2,1,0:T(8,128)S(1)} %bitcast.8, f32[12,16,384]{2,1,0:T(8,128)S(1)} %bitcast.12, f32[3,12,2,16,128]{4,3,2,1,0:T(8,128)S(1)} %get-tuple-element.13.g_ref, f32[2,4,6,16,128]{4,3,2,1,0:T(8,128)S(1)} %get-tuple-element.14.k_ref, f32[1024,384]{1,0:T(8,128)S(1)} %bitcast.9, ...), custom_call_target="tpu_custom_call" | custom-call | tf_op jit(solution)/shard_map/finish/pallas_call | solution.py:538
Async XLA Ops:
  0.0 1.1 %copy-start = (f32[12,1,16,1024]{3,2,1,0:T(8,128)S(1)}, f32[12,1,16,1024]{3,2,1,0:T(8,128)}, u32[]{:S(2)}) copy-start(f32[12,1,16,1024]{3,2,1,0:T(8,128)} %param.2) | copy-start | bytes 2359300
  1.1 1.0 %copy-start.1 = (f32[12,1,16,384]{3,2,1,0:T(8,128)S(1)}, f32[12,1,16,384]{3,2,1,0:T(8,128)}, u32[]{:S(2)}) copy-start(f32[12,1,16,384]{3,2,1,0:T(8,128)} %param.3) | copy-start | bytes 884740

commit v6 on v5

--- a/solution.py
+++ b/solution.py
@@ -138,20 +138,12 @@
         tile = mat_ref[a]
         diag_part = jnp.where(sub > lane, tile, jnp.where(sub == lane, 0.5 * tile, 0.0))
         h_ref[a] = jnp.where(z < a, tile, jnp.where(z == a, diag_part, 0.0))
-    pl.semaphore_wait(barrier, len(peers))
-
-    own_t = pan_ref.at[z]
-    for d in YD:
-        send(own_t, tc_ref.at[x, y, core], t_sems.at[d], to_y(d), OUT_T)
-    for d in XD:
-        send(own_t, tc_ref.at[x, y, core], t_sems.at[NY + d], to_x(d), OUT_T)
+
     tc_ref[x, y, core] = pan_ref[z]
-
     t_rows = pan_ref[...].reshape(NZ * TR, PW)
     gram = dot_tn(t_rows, t_rows)
     for l in range(NL):
         gl_ref[l] = gram[:, l * LW:(l + 1) * LW].reshape(NZ, 2, PW // NZ // 2, LW)
-    send(gl_ref.at[:, z, other], gc_ref, g_sems.at[0], to_core, OUT_G)
     XW = WIDTH // NX
 
     def columns(xb):
@@ -163,6 +155,14 @@
         for c in range(2):
             mpa_ref[c, xb] = terms[:, c, :, :LA]
             mpb_ref[c, :, xb] = terms[:, c, :, LA:]
+    pl.semaphore_wait(barrier, len(peers))
+
+    own_t = pan_ref.at[z]
+    for d in YD:
+        send(own_t, tc_ref.at[x, y, core], t_sems.at[d], to_y(d), OUT_T)
+    for d in XD:
+        send(own_t, tc_ref.at[x, y, core], t_sems.at[NY + d], to_x(d), OUT_T)
+    send(gl_ref.at[:, z, other], gc_ref, g_sems.at[0], to_core, OUT_G)
     send(mpb_ref.at[other], cb_ref, mb_sems.at[0], to_core, OUT_MB)
     send(mpa_ref.at[other], ca_ref, ma_sems.at[0], to_core, OUT_MA)
 

time: 74.5 us -> 73.3 us (0.984)
  Pallas kernels: 72.2 us -> 70.7 us
    pallas_call x1, Pallas kernels: 68.8 us -> 67.3 us  [exchange(): pl.pallas_call(functools.partial(comm_kernel, sizes), out_shape=[shape(NL...]
where the time goes in v6:
time: 73.3 us; the launch traced here: 72.8 us
  Pallas kernels  70.7 us (96%)
  local copies, waits for them, and re-layouts  2.09 us (3%)
    pallas_call x1, Pallas kernels, exchange(): pl.pallas_call(functools.partial(comm_kernel, sizes), out_shape=[shape(NL...  67.3 us
    pallas_call x1, Pallas kernels, finish(): pl.pallas_call(finish_kernel, out_shape=jax.ShapeDtypeStruct(matrix.shape...  3.41 us
    unnamed x4, local copies, waits for them, and re-layouts  2.09 us

profile of v6, /device:TPU:1, one launch (start us, length us, event | category | flops | bytes accessed | tf_op | source)
XLA Modules:
  0.0 72.8 jit_solution(10328051879089911371)
XLA Ops:
  0.0 0.0 copy-start
  0.0 1.1 %copy-done = f32[12,1,16,1024]{3,2,1,0:T(8,128)S(1)} copy-done((f32[12,1,16,1024]{3,2,1,0:T(8,128)S(1)}, f32[12,1,16,1024]{3,2,1,0:T(8,128)}, u32[]{:S(2)}) %copy-start) | copy-done | bytes 786456
  1.1 0.0 copy-start.1
  1.1 1.0 %copy-done.1 = f32[12,1,16,384]{3,2,1,0:T(8,128)S(1)} copy-done((f32[12,1,16,384]{3,2,1,0:T(8,128)S(1)}, f32[12,1,16,384]{3,2,1,0:T(8,128)}, u32[]{:S(2)}) %copy-start.1) | copy-done | bytes 294936
  2.1 67.3 %exchange.1 = (f32[3,12,2,16,128]{4,3,2,1,0:T(8,128)S(1)}, f32[2,4,6,16,128]{4,3,2,1,0:T(8,128)S(1)}, f32[4,8,2,16,384]{4,3,2,1,0:T(8,128)S(1)}, f32[4,8,2,16,38...) custom-call(f32[12,16,1024]{2,1,0:T(8,128)S(1)} %bitcast.7, ...), custom_call_target="tpu_custom_call" | custom-call | tf_op jit(solution)/shard_map/exchange/pallas_call | solution.py:452
  69.4 3.4 %finish.1 = f32[12,16,1024]{2,1,0:T(8,128)} custom-call(f32[12,16,1024]{2,1,0:T(8,128)S(1)} %bitcast.8, f32[12,16,384]{2,1,0:T(8,128)S(1)} %bitcast.12, f32[3,12,2,16,128]{4,3,2,1,0:T(8,128)S(1)} %get-tuple-element.13.g_ref, f32[2,4,6,16,128]{4,3,2,1,0:T(8,128)S(1)} %get-tuple-element.14.k_ref, f32[1024,384]{1,0:T(8,128)S(1)} %bitcast.9, ...), custom_call_target="tpu_custom_call" | custom-call | tf_op jit(solution)/shard_map/finish/pallas_call | solution.py:538
Async XLA Ops:
  0.0 1.1 %copy-start = (f32[12,1,16,1024]{3,2,1,0:T(8,128)S(1)}, f32[12,1,16,1024]{3,2,1,0:T(8,128)}, u32[]{:S(2)}) copy-start(f32[12,1,16,1024]{3,2,1,0:T(8,128)} %param.2) | copy-start | bytes 2359300
  1.1 1.0 %copy-start.1 = (f32[12,1,16,384]{3,2,1,0:T(8,128)S(1)}, f32[12,1,16,384]{3,2,1,0:T(8,128)}, u32[]{:S(2)}) copy-start(f32[12,1,16,384]{3,2,1,0:T(8,128)} %param.3) | copy-start | bytes 884740

commit v7 on v6

--- a/solution.py
+++ b/solution.py
@@ -66,8 +66,8 @@
                 sg_ref, units_ref, h_ref,
                 gl_ref, gc_ref, gsum_ref, gx_ref, gsx_ref, gy_ref,
                 mpa_ref, mpb_ref, ca_ref, cb_ref, ax_ref, ay_ref, by_ref, bs_ref, bx_ref,
-                dp_ref, rz_ref, kp_ref, kc_ref, kx_ref, ks_ref, ky_ref, kz_ref, kf_ref,
-                out_sems, ky_out_sems, t_sems, w_sems, wz_sems, ma_sems, mb_sems, dz_sems,
+                dp_ref, rz_ref, ds_ref, kp_ref, kc_ref, kx_ref, ks_ref, ky_ref, kz_ref, kf_ref,
+                out_sems, ky_out_sems, dz_out_sems, t_sems, w_sems, wz_sems, ma_sems, mb_sems, dz_sems,
                 g_sems, gz_sems, ga_sems, k_sems, kz_sems, ka_sems):
     NX, NY, NZ, TR, WIDTH, PW, NL, LA = sizes
     LW = PW // NL
@@ -244,16 +244,21 @@
     for d in XD:
         send(ks_ref.at[xp(d)], kx_ref.at[d - 1], k_sems.at[d], to_x(d), OUT_K)
 
+    for d in XD:
+        send(mpa_ref.at[core, xp(d)], ax_ref.at[d - 1], ma_sems.at[d], to_x(d), OUT_MA)
+
     for dx in XD:
         xb = xp(NX - dx)
         arrive(tc_ref.at[xb, :, other], t_sems.at[NY + NX + dx])
         direct = direct + dot_split(columns(xb), tc_ref[xb].reshape(XW, PW), NN)
     dp_ref[...] = direct.reshape(NZ, TR, PW)
     for d in ZD:
-        send(dp_ref.at[zp(d)], rz_ref.at[d - 1], dz_sems.at[d - 1], to_z(d), OUT_D)
-
-    for d in XD:
-        send(mpa_ref.at[core, xp(d)], ax_ref.at[d - 1], ma_sems.at[d], to_x(d), OUT_MA)
+        @pl.when(zp(d) > z)
+        def _():
+            pltpu.make_async_remote_copy(
+                src_ref=dp_ref.at[zp(d)], dst_ref=rz_ref.at[d - 1],
+                send_sem=dz_out_sems.at[d - 1], recv_sem=dz_sems.at[d - 1],
+                device_id=to_z(d), device_id_type=pl.DeviceIdType.MESH).start()
 
     ksum = ks_ref[x]
     for d in XD:
@@ -314,10 +319,13 @@
     for d in YD:
         arrive(ay_ref.at[d - 1], ma_sems.at[NX + d])
         part_a = part_a + ay_ref[d - 1]
-    wsum = dp_ref[z]
+    ds_ref[...] = dp_ref[z]
     for d in ZD:
-        arrive(rz_ref.at[d - 1], dz_sems.at[d - 1])
-        wsum = wsum + rz_ref[d - 1]
+        @pl.when(zp(NZ - d) < z)
+        def _():
+            arrive(rz_ref.at[d - 1], dz_sems.at[d - 1])
+            ds_ref[...] += rz_ref[d - 1]
+    wsum = ds_ref[...]
     wr_ref[z, :, :LA] = wsum[:, :LA] + part_a
     wr_ref[z, :, LA:] = wsum[:, LA:] + part_b
     wc_ref[x, y, core] = wr_ref[z]
@@ -418,7 +426,9 @@
         arrive(wc_ref.at[xp(NX - dx), :, other], w_sems.at[NY + NX + dx])
     for dx in [0] + XD:
         arrive(k_ref.at[other, xp(NX - dx)], ka_sems.at[NY + NX + dx])
-    for out in (OUT_T, OUT_W, OUT_MA, OUT_MB, OUT_D, OUT_K):
+    for d in ZD:
+        pl.when(zp(d) > z)(functools.partial(left, rz_ref.at[d - 1], dz_out_sems.at[d - 1]))
+    for out in (OUT_T, OUT_W, OUT_MA, OUT_MB, OUT_K):
         all_left(out)
     left(g_ref.at[:, :, core], out_sems.at[OUT_GC])
     left(kx_ref, out_sems.at[OUT_KX])
@@ -463,9 +473,9 @@
             V(2, NX, NY, TR, LA), V(2, NY, NX, TR, LB), V(NX, NY, TR, LA), V(NY, NX, TR, LB),
             V(NX - 1, NY, TR, LA), V(NY - 1, TR, LA), V(NY - 1, NX, TR, LB), V(NX, TR, LB),
             V(NX - 1, TR, LB),
-            V(NZ, TR, PW), V(NZ - 1, TR, PW), V(2, NX, NP, KR, LW), V(NX, NP, KR, LW),
+            V(NZ, TR, PW), V(NZ - 1, TR, PW), V(TR, PW), V(2, NX, NP, KR, LW), V(NX, NP, KR, LW),
             V(NX - 1, NP, KR, LW), V(NX, NP, KR, LW), V(NY - 1, KR, LW), V(NZ - 1, KR, LW), V(KR, LW),
-            D(13), D(NY + NX), D(NY + 2 * NX), D(NY + 2 * NX), D(NZ - 1), D(NX + NY), D(NX + NY),
+            D(13), D(NY + NX), D(NZ - 1), D(NY + 2 * NX), D(NY + 2 * NX), D(NZ - 1), D(NX + NY), D(NX + NY),
             D(NZ - 1), D(NX + NY), D(NZ - 1), D(NX), D(NX + NY), D(NZ - 1), D(2 * NX + NY),
         ],
         compiler_params=pltpu.CompilerParams(

time: 73.3 us -> 73.7 us (level)
  no operation moved by 1% of the time
where the time goes in v7:
time: 73.7 us; the launch traced here: 73.5 us
  Pallas kernels  71.4 us (97%)
  local copies, waits for them, and re-layouts  2.09 us (3%)
    pallas_call x1, Pallas kernels, exchange(): pl.pallas_call(functools.partial(comm_kernel, sizes), out_shape=[shape(NL...  68 us
    pallas_call x1, Pallas kernels, finish(): pl.pallas_call(finish_kernel, out_shape=jax.ShapeDtypeStruct(matrix.shape...  3.4 us
    unnamed x4, local copies, waits for them, and re-layouts  2.09 us

profile of v7, /device:TPU:1, one launch (start us, length us, event | category | flops | bytes accessed | tf_op | source)
XLA Modules:
  0.0 73.5 jit_solution(52549616206558531)
XLA Ops:
  0.0 0.0 copy-start
  0.0 1.1 %copy-done = f32[12,1,16,1024]{3,2,1,0:T(8,128)S(1)} copy-done((f32[12,1,16,1024]{3,2,1,0:T(8,128)S(1)}, f32[12,1,16,1024]{3,2,1,0:T(8,128)}, u32[]{:S(2)}) %copy-start) | copy-done | bytes 786456
  1.1 0.0 copy-start.1
  1.1 1.0 %copy-done.1 = f32[12,1,16,384]{3,2,1,0:T(8,128)S(1)} copy-done((f32[12,1,16,384]{3,2,1,0:T(8,128)S(1)}, f32[12,1,16,384]{3,2,1,0:T(8,128)}, u32[]{:S(2)}) %copy-start.1) | copy-done | bytes 294936
  2.1 68.0 %exchange.1 = (f32[3,12,2,16,128]{4,3,2,1,0:T(8,128)S(1)}, f32[2,4,6,16,128]{4,3,2,1,0:T(8,128)S(1)}, f32[4,8,2,16,384]{4,3,2,1,0:T(8,128)S(1)}, f32[4,8,2,16,38...) custom-call(f32[12,16,1024]{2,1,0:T(8,128)S(1)} %bitcast.7, ...), custom_call_target="tpu_custom_call" | custom-call | tf_op jit(solution)/shard_map/exchange/pallas_call | solution.py:462
  70.1 3.4 %finish.1 = f32[12,16,1024]{2,1,0:T(8,128)} custom-call(f32[12,16,1024]{2,1,0:T(8,128)S(1)} %bitcast.8, f32[12,16,384]{2,1,0:T(8,128)S(1)} %bitcast.12, f32[3,12,2,16,128]{4,3,2,1,0:T(8,128)S(1)} %get-tuple-element.13.g_ref, f32[2,4,6,16,128]{4,3,2,1,0:T(8,128)S(1)} %get-tuple-element.14.k_ref, f32[1024,384]{1,0:T(8,128)S(1)} %bitcast.9, ...), custom_call_target="tpu_custom_call" | custom-call | tf_op jit(solution)/shard_map/finish/pallas_call | solution.py:548
Async XLA Ops:
  0.0 1.1 %copy-start = (f32[12,1,16,1024]{3,2,1,0:T(8,128)S(1)}, f32[12,1,16,1024]{3,2,1,0:T(8,128)}, u32[]{:S(2)}) copy-start(f32[12,1,16,1024]{3,2,1,0:T(8,128)} %param.2) | copy-start | bytes 2359300
  1.1 1.0 %copy-start.1 = (f32[12,1,16,384]{3,2,1,0:T(8,128)S(1)}, f32[12,1,16,384]{3,2,1,0:T(8,128)}, u32[]{:S(2)}) copy-start(f32[12,1,16,384]{3,2,1,0:T(8,128)} %param.3) | copy-start | bytes 884740
